TPU v7x, 256 devices: a whole 4x4x8 slice. The times are simulated.
256 devices in a mesh: wide: 128 (over x, y, z_lo, core), section: 2 (over z_hi).
Axes of the slice: x: 4, y: 4, z: 8 (z_hi: 2, z_lo: 4; z = z_hi * 4 + z_lo), core: 2. Of those that a mesh axis runs over, the one named last changes fastest.
Arguments:
- potential: float32 [4, 512, 16384], P('section', 'wide'), may hold values from -6 to 6
- speed_x: float32 [512, 16384], P('wide'), may hold values from 0.5 to 2
- speed_y: float32 [512, 16384], P('wide'), may hold values from 0.5 to 2
- density: float32 [512, 16384], P('wide'), may hold values from 0 to 2
- sign_x: int32 [4, 512, 16384], P('section', 'wide'), may hold values 0 or 1
- sign_y: int32 [4, 512, 16384], P('section', 'wide'), may hold values 0 or 1
- stem_weight: bfloat16 [45, 128], replicated, may hold values from -0.875 to 0.875
- conv_weight: bfloat16 [1, 3, 128], replicated, may hold values from -3.5 to 3.5
- norm_gain: float32 [1, 128], replicated, may hold values from 0.1 to 1.9
- up_weight: bfloat16 [1, 128, 256], replicated, may hold values from -0.5 to 0.5
- down_weight: bfloat16 [1, 256, 128], replicated, may hold values from -0.375 to 0.375
- out_weight: bfloat16 [128, 4], replicated, may hold values from -0.5 to 0.5
Outputs:
- corrected: float32 [4, 512, 16384], P(None, ('wide', 'section'))
All inputs are finite; a program needn't handle non-finite values. No bound on the sum of `sign_x` or of `sign_y` on one device may be relied on, other than what follows from the above.
Results may differ from a plain program's by a relative error of at most 0.003.
Values may be sent and summed in bfloat16 or wider, within the bound.
No kernel may reach another device: no remote copies, remote signals or barrier semaphores. Data moves between devices by JAX's collectives and lax.ppermute only.
A program may use at most 64 MiB of HBM per device.

v0:
```python
import jax
import jax.numpy as jnp
from jax import lax
from jax.sharding import PartitionSpec as P

CENTRAL = (1.0 / 280.0, -4.0 / 105.0, 0.2, -0.8, 0.0, 0.8, -0.2, 4.0 / 105.0, -1.0 / 280.0)
BINOMIAL = (1.0, -8.0, 28.0, -56.0, 70.0, -56.0, 28.0, -8.0, 1.0)
DAMPING = 1.0 / 630.0
TIME_STEP = 0.6
EPSILON = 1e-06


def extended_2(value, sides, width):
    for axis, dim in sides:
        size, length = (lax.axis_size(axis), value.shape[dim])
        up = [(i, (i + 1) % size) for i in range(size - 1)]
        down = [(j, i) for i, j in up]
        last = lax.slice_in_dim(value, length - width, length, axis=dim)
        initial = lax.slice_in_dim(value, 0, width, axis=dim)
        before = lax.ppermute(last, axis, up)
        after = lax.ppermute(initial, axis, down)
        value = jnp.concatenate([before, value, after], axis=dim)
    return value


def banded_valid(extended, along, length):
    window = lax.slice_in_dim(extended, 0, length, axis=along)
    central = CENTRAL[0] * window
    damping = BINOMIAL[0] * window
    for offset in range(1, 9):
        window = lax.slice_in_dim(extended, offset, offset + length, axis=along)
        central = central + CENTRAL[offset] * window
        damping = damping + BINOMIAL[offset] * window
    return (central, damping)


def banded(source, along):
    widths = [(0, 0)] * source.ndim
    widths[along] = (4, 4)
    return banded_valid(jnp.pad(source, widths), along, source.shape[along])


def upwind(source, central, damping, signs, speeds):
    gradient = central + (2.0 * signs - 1.0) * DAMPING * damping
    return source - TIME_STEP * speeds * gradient


def product(left, right):
    return jnp.dot(
        left.astype(jnp.float32), right.astype(jnp.float32), preferred_element_type=jnp.float32
    )


def correct_row(window, stem_weight, conv_weight, norm_gain, up_weight, down_weight, out_weight):
    count = window.shape[2] - 2
    pieces = [
        window[:, row_shift, col_shift : col_shift + count]
        for row_shift in range(3)
        for col_shift in range(3)
    ]
    patches = jnp.transpose(jnp.concatenate(pieces, axis=0))
    hidden = product(patches, stem_weight)
    kernel = conv_weight[0].astype(jnp.float32)
    padded = jnp.pad(hidden, ((1, 1), (0, 0)))
    mixed_rows = kernel[0] * padded[:-2] + kernel[1] * padded[1:-1] + kernel[2] * padded[2:]
    inverse_rms = lax.rsqrt(jnp.mean(mixed_rows * mixed_rows, axis=-1, keepdims=True) + EPSILON)
    normed = (mixed_rows * inverse_rms * norm_gain[0]).astype(jnp.bfloat16)
    lifted = jax.nn.gelu(product(normed, up_weight[0])).astype(jnp.bfloat16)
    hidden = hidden + product(lifted, down_weight[0])
    return jnp.transpose(product(hidden.astype(jnp.bfloat16), out_weight))


def shards(
    potential,
    speed_x,
    speed_y,
    density,
    sign_x,
    sign_y,
    stem_weight,
    conv_weight,
    norm_gain,
    up_weight,
    down_weight,
    out_weight,
):
    central, damping = banded(potential, 2)
    swept_x = upwind(potential, central, damping, sign_x.astype(jnp.float32), speed_x[None])
    col_central, col_damping = banded(
        lax.all_to_all(swept_x, "wide", split_axis=2, concat_axis=1, tiled=True), 1
    )
    central = lax.all_to_all(col_central, "wide", split_axis=1, concat_axis=2, tiled=True)
    damping = lax.all_to_all(col_damping, "wide", split_axis=1, concat_axis=2, tiled=True)
    swept_y = upwind(swept_x, central, damping, sign_y.astype(jnp.float32), speed_y[None])
    physics = swept_y + TIME_STEP * density[None]
    own_slab = lax.all_to_all(physics, "section", split_axis=1, concat_axis=0, tiled=True)
    half_rows = own_slab.shape[1]
    section_pos = lax.axis_index("section")
    own_density = lax.dynamic_slice_in_dim(density, section_pos * half_rows, half_rows, 0)
    features = jnp.concatenate([own_slab, own_density[None]], axis=0).astype(jnp.bfloat16)
    with_rims = extended_2(features, ((("wide", "section"), 1),), 1)
    padded = jnp.pad(with_rims, ((0, 0), (0, 0), (1, 1)))

    def one_row(row_index):
        window = lax.dynamic_slice_in_dim(padded, row_index, 3, 1)
        return correct_row(
            window, stem_weight, conv_weight, norm_gain, up_weight, down_weight, out_weight
        )

    corrections = lax.map(one_row, jnp.arange(half_rows, dtype=jnp.int32))
    return own_slab + jnp.transpose(corrections, (1, 0, 2))


def solution(mesh):
    placed = (
        P("section", "wide", None),
        P("wide", None),
        P("wide", None),
        P("wide", None),
        P("section", "wide", None),
        P("section", "wide", None),
        P(),
        P(),
        P(),
        P(),
        P(),
        P(),
    )
    return jax.shard_map(
        shards,
        mesh=mesh,
        in_specs=placed,
        out_specs=P(None, ("wide", "section"), None),
        check_vma=False,
    )
```

profile of v0, /device:TPU:32, one launch (start us, length us, event | category | flops | bytes accessed | tf_op | source)
XLA Modules:
  0.0 372.8 jit_solution(1504831351970332186)
XLA Ops:
  0.0 1.0 broadcast_multiply_fusion.2
  1.0 5.5 %multiply_subtract_fusion = f32[2,4,16384]{2,1,0:T(4,128)S(1)} fusion(f32[2,4,16384]{2,1,0:T(4,128)} %param.14, s32[2,4,16384]{2,1,0:T(4,128)} %param.18, f32[4,16384]{1,0:T(4,128)S(1)} %broadcast_multiply_fusion.2), kind=kLoop, calls=%fused_computation.58 | loop fusion | flops 5242880 | bytes 1835008 | tf_op jit(solution)/shard_map/sub | solution.py:45
  6.5 14.9 %copy.61 = f32[2,4,16384]{1,0,2:T(2,128)} copy(f32[2,4,16384]{2,1,0:T(4,128)S(1)} %multiply_subtract_fusion) | data formatting | bytes 1048576 | tf_op jit(solution)/shard_map/sub | solution.py:45
  21.4 27.0 %reshape.22 = f32[128,1,1024]{2,1,0:T(1,128)S(1)} reshape(f32[16384,2,4]{2,1,0:T(2,128)} %bitcast.99) | data formatting | bytes 1048576
  48.4 29.9 %all_to_all.72 = f32[128,1,1024]{2,1,0:T(1,128)S(1)} all-to-all(f32[128,1,1024]{2,1,0:T(1,128)S(1)} %reshape.22), channel_id=1, replica_groups=mesh['wide'=128,'section'=2] {'wide'}, dimensions={0} | all-to-all | bytes 1048576 | tf_op jit(solution)/shard_map/all_to_all | solution.py:90
  78.8 1.9 reduce
  80.7 27.3 %reshape.23 = f32[16384,2,4]{2,1,0:T(2,128)} reshape(f32[128,1024]{1,0:T(8,128)S(1)} %reduce) | data formatting | bytes 1048576
  108.0 17.9 %copy.62 = f32[2,4,128,128]{3,1,2,0:T(4,128)S(1)} copy(f32[2,4,128,128]{1,0,3,2:T(2,128)} %bitcast.98) | data formatting | bytes 1048576 | tf_op jit(solution)/shard_map/all_to_all | solution.py:90
  125.9 0.8 add_add_fusion
  126.7 1.2 copy.63
  127.9 7.7 %all-to-all-start.1 = ((f32[2,512,128]{2,0,1:T(2,128)}), f32[2,512,128]{2,0,1:T(2,128)S(1)}, u32[]{:S(2)}, u32[]{:S(2)}) async-start(f32[2,512,128]{2,0,1:T(2,128)} %copy.63), calls=%async_computation.1 | async-start | bytes 1048576 | tf_op jit(solution)/shard_map/all_to_all | solution.py:92
  135.6 1.2 copy.65
  136.8 16.4 %all-to-all-done.1 = f32[2,512,128]{2,0,1:T(2,128)S(1)} async-done(((f32[2,512,128]{2,0,1:T(2,128)}), f32[2,512,128]{2,0,1:T(2,128)S(1)}, u32[]{:S(2)}, u32[]{:S(2)}) %all-to-all-start.1) | async-done | bytes 524320 | tf_op jit(solution)/shard_map/all_to_all | solution.py:92
  153.2 7.5 %all-to-all-start.2 = ((f32[2,512,128]{2,0,1:T(2,128)}), f32[2,512,128]{2,0,1:T(2,128)S(1)}, u32[]{:S(2)}, u32[]{:S(2)}) async-start(f32[2,512,128]{2,0,1:T(2,128)} %copy.65), calls=%async_computation.2 | async-start | bytes 1048576 | tf_op jit(solution)/shard_map/all_to_all | solution.py:93
  160.9 17.4 %all-to-all-done.2 = f32[2,512,128]{2,0,1:T(2,128)S(1)} async-done(((f32[2,512,128]{2,0,1:T(2,128)}), f32[2,512,128]{2,0,1:T(2,128)S(1)}, u32[]{:S(2)}, u32[]{:S(2)}) %all-to-all-start.2) | async-done | bytes 524320 | tf_op jit(solution)/shard_map/all_to_all | solution.py:93
  178.7 1.2 copy.67
  179.9 5.8 %all-to-all-start.3 = ((f32[2,4,16384]{2,0,1:T(2,128)}), f32[2,4,16384]{2,0,1:T(2,128)S(1)}, u32[]{:S(2)}, u32[]{:S(2)}) async-start(f32[2,4,16384]{2,0,1:T(2,128)} %copy.67), calls=%async_computation.3 | async-start | bytes 1048576 | tf_op jit(solution)/shard_map/all_to_all | solution.py:96
  185.7 17.6 %all-to-all-done.3 = f32[2,4,16384]{2,0,1:T(2,128)S(1)} async-done(((f32[2,4,16384]{2,0,1:T(2,128)}), f32[2,4,16384]{2,0,1:T(2,128)S(1)}, u32[]{:S(2)}, u32[]{:S(2)}) %all-to-all-start.3) | async-done | bytes 524320 | tf_op jit(solution)/shard_map/all_to_all | solution.py:96
  203.8 0.8 copy-done.1
  205.4 2.4 collective-permute-start
  207.9 6.1 %collective-permute-start.1 = (bf16[5,1,16384]{2,1,0:T(2,128)(2,1)S(1)}, bf16[5,1,16384]{2,1,0:T(2,128)(2,1)S(1)}, u32[]{:S(2)}, u32[]{:S(2)}) collective-permute-start(bf16[5,1,16384]{2,1,0:T(2,128)(2,1)S(1)} %get-tuple-element.204), channel_id=1, source_target_pairs={{1,0},{2,1},{3,2},{4,3},{5,4},{6,5},{7,6},{8,7},{9,8},{10,9},{11,1... | collective-permute-start | bytes 491528 | tf_op jit(solution)/shard_map/ppermute | solution.py:21
  214.0 27.2 %collective-permute-done = bf16[5,1,16384]{2,1,0:T(2,128)(2,1)S(1)} collective-permute-done((bf16[5,1,16384]{2,1,0:T(2,128)(2,1)S(1)}, bf16[5,1,16384]{2,1,0:T(2,128)(2,1)S(1)}, u32[]{:S(2)}, u32[]{:S(2)}) %collective-permute-start) | collective-permute-done | bytes 163872 | tf_op jit(solution)/shard_map/ppermute | solution.py:20
  241.3 1.8 select_maximum_fusion
  243.6 126.9 %while.12 = (s32[]{:T(128)}, f32[2,4,16384]{2,0,1:T(2,128)}, s32[2]{0:T(128)}, bf16[5,4,16386]{2,1,0:T(4,128)(2,1)S(1)}, bf16[45,128]{1,0:T(8,128)(2,1)}, /*inde...) while((s32[]{:T(128)}, f32[2,4,16384]{2,0,1:T(2,128)}, ...), condition=%wide.region_2.3_spmd, body=%wide.region_0.2_spmd.sunk | while | flops 2426421760 | bytes 92265896 | solution.py:110
  243.6 1.2 dynamic_slice.21
  246.7 4.3 %constant_dynamic-slice_fusion.10 = (bf16[5,1,16384]{2,1,0:T(2,128)(2,1)S(1)}, bf16[5,1,16384]{2,1,0:T(2,128)(2,1)S(1)}, bf16[5,1,16384]{2,1,0:T(2,128)(2,1)S(1)...) fusion(bf16[5,4,16386]{2,1,0:T(4,128)(2,1)S(1)} %get-tuple-elem, ...), kind=kLoop, calls=%fused_computation.37.clone.1 | loop fusion | bytes 2949140 | tf_op jit(solution)/shard_map/while/body/eval_jaxpr/slice | solution.py:57
  251.8 1.2 copy_bitcast_fusion.14
  253.0 1.2 copy_bitcast_fusion.13
  254.4 13.7 %concatenate.16 = bf16[45,16384]{1,0:T(8,128)(2,1)S(1)} concatenate(bf16[5,16384]{1,0:T(8,128)(2,1)S(1)} %bitcast.100, bf16[5,16384]{1,0:T(8,128)(2,1)} %get-tuple-element.291, bf16[5,16384]{1,0:T(8,128)(2,1)} %get-tuple-element.292, bf16[5,16384]{1,0:T(8,128)(2,1)} %get-tuple-element.295, bf16[5,16384]{1,0:T(8,128)(2,1)} %get-tuple-element.296, ...), dimensions={0} | concatenate | bytes 2949120 | tf_op jit(solution)/shard_map/while/body/eval_jaxpr/concatenate | solution.py:61
  268.1 2.1 fusion.42
  270.2 3.2 copy-done
  273.4 3.5 multiply_reduce_fusion.2
  277.0 22.3 %fusion.43 = bf16[16384,128]{1,0:T(8,128)(2,1)} fusion(f32[16384,128]{1,0:T(8,128)} %copy-done, f32[128]{0:T(128)S(1)} %bitcast.105, f32[16384]{0:T(1024)S(1)} %add_rsqrt_fusion.2, bf16[1,256,128]{2,1,0:T(8,128)(2,1)S(1)} %copy-done.10, bf16[1,128,256]{2,1,0:T(8,128)(2,1)S(1)} %copy-done.9, f32[128]{0:T(128)S(1)} %get-tuple-element.305, ...), kind=kOutput, calls=%fused_computation.2.clone.1 | convolution fusion | flops 2206203904 | bytes 21170176 | tf_op jit(solution)/shard_map/while/body/eval_jaxpr/dot_general | solution.py:49
  299.3 3.4 convolution_bitcast_fusion.2
  302.9 3.3 dynamic_update_slice.8
  306.3 0.8 copy-done.3
  307.1 1.2 dynamic_slice.21
  310.2 4.3 %constant_dynamic-slice_fusion.10 = (bf16[5,1,16384]{2,1,0:T(2,128)(2,1)S(1)}, bf16[5,1,16384]{2,1,0:T(2,128)(2,1)S(1)}, bf16[5,1,16384]{2,1,0:T(2,128)(2,1)S(1)...) fusion(bf16[5,4,16386]{2,1,0:T(4,128)(2,1)S(1)} %get-tuple-elem, ...), kind=kLoop, calls=%fused_computation.37.clone.1 | loop fusion | bytes 2949140 | tf_op jit(solution)/shard_map/while/body/eval_jaxpr/slice | solution.py:57
  315.3 1.2 copy_bitcast_fusion.14
  316.5 1.2 copy_bitcast_fusion.13
  317.8 13.7 %concatenate.16 = bf16[45,16384]{1,0:T(8,128)(2,1)S(1)} concatenate(bf16[5,16384]{1,0:T(8,128)(2,1)S(1)} %bitcast.100, bf16[5,16384]{1,0:T(8,128)(2,1)} %get-tuple-element.291, bf16[5,16384]{1,0:T(8,128)(2,1)} %get-tuple-element.292, bf16[5,16384]{1,0:T(8,128)(2,1)} %get-tuple-element.295, bf16[5,16384]{1,0:T(8,128)(2,1)} %get-tuple-element.296, ...), dimensions={0} | concatenate | bytes 2949120 | tf_op jit(solution)/shard_map/while/body/eval_jaxpr/concatenate | solution.py:61
  331.6 2.1 fusion.42
  333.7 3.2 copy-done
  336.9 3.5 multiply_reduce_fusion.2
  340.5 22.3 %fusion.43 = bf16[16384,128]{1,0:T(8,128)(2,1)} fusion(f32[16384,128]{1,0:T(8,128)} %copy-done, f32[128]{0:T(128)S(1)} %bitcast.105, f32[16384]{0:T(1024)S(1)} %add_rsqrt_fusion.2, bf16[1,256,128]{2,1,0:T(8,128)(2,1)S(1)} %copy-done.10, bf16[1,128,256]{2,1,0:T(8,128)(2,1)S(1)} %copy-done.9, f32[128]{0:T(128)S(1)} %get-tuple-element.305, ...), kind=kOutput, calls=%fused_computation.2.clone.1 | convolution fusion | flops 2206203904 | bytes 21170176 | tf_op jit(solution)/shard_map/while/body/eval_jaxpr/dot_general | solution.py:49
  362.7 3.4 convolution_bitcast_fusion.2
  366.4 3.3 dynamic_update_slice.8
  370.5 2.3 bitcast_add_fusion
  (58 shorter events, 6.3 us)
Async XLA Ops:
  108.0 52.7 %copy-start.5 = (f32[4,16384]{1,0:T(4,128)S(1)}, f32[4,16384]{1,0:T(4,128)}, u32[]{:S(2)}) copy-start(f32[4,16384]{1,0:T(4,128)} %param.17) | copy-start | bytes 786436
  108.0 52.7 %copy-start.6 = (f32[4,16384]{1,0:T(4,128)S(1)}, f32[4,16384]{1,0:T(4,128)}, u32[]{:S(2)}) copy-start(f32[4,16384]{1,0:T(4,128)} %param.16) | copy-start | bytes 786436
  125.9 52.4 %copy-start.4 = (s32[2,4,16384]{2,1,0:T(4,128)S(1)}, s32[2,4,16384]{2,1,0:T(4,128)}, u32[]{:S(2)}) copy-start(s32[2,4,16384]{2,1,0:T(4,128)} %param.19) | copy-start | bytes 1572868
  126.7 116.9 %copy-start.7 = (bf16[128,4]{0,1:T(4,128)(2,1)S(1)}, bf16[128,4]{0,1:T(4,128)(2,1)}, u32[]{:S(2)}) copy-start(bf16[128,4]{0,1:T(4,128)(2,1)} %param.25) | copy-start | bytes 3076
  126.7 116.9 %copy-start.8 = (bf16[1,3,128]{2,1,0:T(4,128)(2,1)S(1)}, bf16[1,3,128]{2,1,0:T(4,128)(2,1)}, u32[]{:S(2)}) copy-start(bf16[1,3,128]{2,1,0:T(4,128)(2,1)} %param.21) | copy-start | bytes 2308
  127.9 25.3 %all-to-all-start.1 = ((f32[2,512,128]{2,0,1:T(2,128)}), f32[2,512,128]{2,0,1:T(2,128)S(1)}, u32[]{:S(2)}, u32[]{:S(2)}) async-start(f32[2,512,128]{2,0,1:T(2,128)} %copy.63), calls=%async_computation.1 | async-start | bytes 1048576 | tf_op jit(solution)/shard_map/all_to_all | solution.py:92
  153.2 25.1 %all-to-all-start.2 = ((f32[2,512,128]{2,0,1:T(2,128)}), f32[2,512,128]{2,0,1:T(2,128)S(1)}, u32[]{:S(2)}, u32[]{:S(2)}) async-start(f32[2,512,128]{2,0,1:T(2,128)} %copy.65), calls=%async_computation.2 | async-start | bytes 1048576 | tf_op jit(solution)/shard_map/all_to_all | solution.py:93
  179.9 23.5 %all-to-all-start.3 = ((f32[2,4,16384]{2,0,1:T(2,128)}), f32[2,4,16384]{2,0,1:T(2,128)S(1)}, u32[]{:S(2)}, u32[]{:S(2)}) async-start(f32[2,4,16384]{2,0,1:T(2,128)} %copy.67), calls=%async_computation.3 | async-start | bytes 1048576 | tf_op jit(solution)/shard_map/all_to_all | solution.py:96
  203.8 0.8 copy-start.1
  205.4 35.8 %collective-permute-start = (bf16[5,1,16384]{2,1,0:T(2,128)(2,1)S(1)}, bf16[5,1,16384]{2,1,0:T(2,128)(2,1)S(1)}, u32[]{:S(2)}, u32[]{:S(2)}) collective-permute-start(bf16[5,1,16384]{2,1,0:T(2,128)(2,1)S(1)} %get-tuple-element.203), channel_id=1, source_target_pairs={{0,1},{1,2},{2,3},{3,4},{4,5},{5,6},{6,7},{7,8},{8,9},{9,10},{10,1... | collective-permute-start | bytes 491528 | tf_op jit(solution)/shard_map/ppermute | solution.py:20
  207.9 33.4 %collective-permute-start.1 = (bf16[5,1,16384]{2,1,0:T(2,128)(2,1)S(1)}, bf16[5,1,16384]{2,1,0:T(2,128)(2,1)S(1)}, u32[]{:S(2)}, u32[]{:S(2)}) collective-permute-start(bf16[5,1,16384]{2,1,0:T(2,128)(2,1)S(1)} %get-tuple-element.204), channel_id=1, source_target_pairs={{1,0},{2,1},{3,2},{4,3},{5,4},{6,5},{7,6},{8,7},{9,8},{10,9},{11,1... | collective-permute-start | bytes 491528 | tf_op jit(solution)/shard_map/ppermute | solution.py:21
  268.1 8.9 %copy-start.9 = (bf16[1,128,256]{2,1,0:T(8,128)(2,1)S(1)}, bf16[1,128,256]{2,1,0:T(8,128)(2,1)}, u32[]{:S(2)}) copy-start(bf16[1,128,256]{2,1,0:T(8,128)(2,1)} %get-tuple-element.345) | copy-start | bytes 196612 | tf_op jit(solution)/shard_map/while
  268.1 8.9 %copy-start.10 = (bf16[1,256,128]{2,1,0:T(8,128)(2,1)S(1)}, bf16[1,256,128]{2,1,0:T(8,128)(2,1)}, u32[]{:S(2)}) copy-start(bf16[1,256,128]{2,1,0:T(8,128)(2,1)} %get-tuple-element.346) | copy-start | bytes 196612 | tf_op jit(solution)/shard_map/while
  268.1 8.9 %copy-start.11 = (f32[1,128]{1,0:T(1,128)S(1)}, f32[1,128]{1,0:T(1,128)}, u32[]{:S(2)}) copy-start(f32[1,128]{1,0:T(1,128)} %get-tuple-element.344) | copy-start | bytes 1540 | tf_op jit(solution)/shard_map/while
  270.2 3.2 copy-start
  277.0 25.9 %copy-start.2 = (f32[2,4,16384]{2,0,1:T(2,128)S(1)}, f32[2,4,16384]{2,0,1:T(2,128)}, u32[]{:S(2)}) copy-start(f32[2,4,16384]{2,0,1:T(2,128)} %get-tuple-element.324) | copy-start | bytes 1572868 | tf_op jit(solution)/shard_map/while
  306.3 0.8 copy-start.3
  331.5 8.9 %copy-start.9 = (bf16[1,128,256]{2,1,0:T(8,128)(2,1)S(1)}, bf16[1,128,256]{2,1,0:T(8,128)(2,1)}, u32[]{:S(2)}) copy-start(bf16[1,128,256]{2,1,0:T(8,128)(2,1)} %get-tuple-element.345) | copy-start | bytes 196612 | tf_op jit(solution)/shard_map/while
  331.5 8.9 %copy-start.10 = (bf16[1,256,128]{2,1,0:T(8,128)(2,1)S(1)}, bf16[1,256,128]{2,1,0:T(8,128)(2,1)}, u32[]{:S(2)}) copy-start(bf16[1,256,128]{2,1,0:T(8,128)(2,1)} %get-tuple-element.346) | copy-start | bytes 196612 | tf_op jit(solution)/shard_map/while
  331.6 8.9 %copy-start.11 = (f32[1,128]{1,0:T(1,128)S(1)}, f32[1,128]{1,0:T(1,128)}, u32[]{:S(2)}) copy-start(f32[1,128]{1,0:T(1,128)} %get-tuple-element.344) | copy-start | bytes 1540 | tf_op jit(solution)/shard_map/while
  333.6 3.2 copy-start
  340.5 25.9 %copy-start.2 = (f32[2,4,16384]{2,0,1:T(2,128)S(1)}, f32[2,4,16384]{2,0,1:T(2,128)}, u32[]{:S(2)}) copy-start(f32[2,4,16384]{2,0,1:T(2,128)} %get-tuple-element.324) | copy-start | bytes 1572868 | tf_op jit(solution)/shard_map/while
  369.7 0.8 copy-start.3
where the time goes:
time: 375 us; the launch traced here: 373 us
  local copies, waits for them, and re-layouts  154 us (41%)
  waiting for transfers between devices  78.7 us (21%)
  matrix products  55.3 us (15%)
  blocking collectives  29.9 us (8%)
  starting transfers between devices  29.5 us (8%)
  other arithmetic  21.6 us (6%)
  loops' own time  4.09 us (1%)
    dot_general x6, matrix products, product(): jnp.dot(left.astype(jnp.float32), right.astype(jnp.float32), preferred_el...  55.3 us
    unnamed x14, local copies, waits for them, and re-layouts  55.2 us
    all_to_all x1, blocking collectives, shards(): lax.all_to_all(swept_x, 'wide', split_axis=2, concat_axis=1, tiled=True)  29.9 us
    concatenate x2, local copies, waits for them, and re-layouts, correct_row(): patches = jnp.transpose(jnp.concatenate(pieces, axis=0))  27.4 us
    ppermute x1, waiting for transfers between devices, extended_2(): before = lax.ppermute(last, axis, up)  27.2 us
    all_to_all x2, local copies, waits for them, and re-layouts, shards(): lax.all_to_all(swept_x, 'wide', split_axis=2, concat_axis=1, tiled=True)  18.4 us
    all_to_all x1, waiting for transfers between devices, shards(): lax.all_to_all(physics, 'section', split_axis=1, concat_axis=0, tiled=True)  17.6 us
    all_to_all x1, waiting for transfers between devices, shards(): lax.all_to_all(col_damping, 'wide', split_axis=1, concat_axis=2, tiled=True)  17.4 us
  transfers between devices with their start and end apart: 5, of which 4 were waited for; matrix products, arithmetic and copies ran while one was open for 0% of the time, Pallas kernels for 0%

commit v1 on v0

v1 whole, which is shorter than its diff:
```python
import functools

import jax
import jax.numpy as jnp
from jax import lax
from jax.experimental import pallas as pl
from jax.experimental.pallas import tpu as pltpu
from jax.sharding import PartitionSpec as P

CENTRAL = (0.8, -0.2, 4.0 / 105.0, -1.0 / 280.0)
BINOMIAL = (70.0, -56.0, 28.0, -8.0, 1.0)
DAMPING = 1.0 / 630.0
TIME_STEP = 0.6
EPSILON = 1e-06
GELU_0 = 0.7978845608028654
GELU_1 = GELU_0 * 0.044715
BF16 = jnp.bfloat16
F32 = jnp.float32
BOTH = ("wide", "section")
HALO = 128


def steps(length, size, body):
    def step(index, carry):
        body(pl.multiple_of(index * size, size))
        return carry

    lax.fori_loop(0, length // size, step, 0)


def upwind_change(center, pairs, signs, speeds):
    central = jnp.zeros_like(center)
    damping = BINOMIAL[0] * center
    for k, (before, after) in enumerate(pairs, 1):
        central = central + CENTRAL[k - 1] * (after - before)
        damping = damping + BINOMIAL[k] * (after + before)
    gradient = central + (2.0 * signs - 1.0) * (DAMPING * damping)
    return (TIME_STEP * speeds) * gradient


def stacked(first, second):
    return jnp.concatenate([first, second], axis=0)


def by_row(value, row):
    roll = functools.partial(pltpu.roll, axis=0)
    placed = value
    for r in range(1, 4):
        placed = jnp.where(row == 2 * r, roll(value, r), placed)
        placed = jnp.where(row == 2 * r - 1, roll(value, 4 + r), placed)
    return placed


def sweep_x(size, pot_ref, speed_ref, sign_ref, wide_ref, narrow_ref, padded):
    length = pot_ref.shape[2]
    padded[:, :HALO] = jnp.zeros((8, HALO), F32)
    padded[:, HALO + length :] = jnp.zeros((8, HALO), F32)
    padded[0:4, HALO : HALO + length] = pot_ref[0]
    padded[4:8, HALO : HALO + length] = pot_ref[1]

    def body(start):
        here = pl.ds(start, size)
        value = padded[:, pl.ds(start, size + 2 * HALO)]
        sign = stacked(sign_ref[0, :, here], sign_ref[1, :, here]).astype(F32)
        speed = stacked(speed_ref[:, here], speed_ref[:, here])

        def at(k):
            return value[:, HALO + k : HALO + k + size]

        swept = at(0) - upwind_change(at(0), [(at(-k), at(k)) for k in range(1, 5)], sign, speed)
        wide_ref[:, here] = swept
        narrow_ref[:, here] = swept.astype(BF16)

    steps(length, size, body)


def sweep_y(
    size,
    own_ref,
    chip_ref,
    far_ref,
    speed_ref,
    sign_ref,
    density_ref,
    own_rows_ref,
    inner_ref,
    outer_ref,
    swap_ref,
    edge_ref,
    cross_ref,
):
    odd = lax.rem(lax.axis_index("wide"), 2) == 1
    low = lax.axis_index("section") == 0

    def body(start):
        here = pl.ds(start, size)
        own, chip, far = own_ref[:, here], chip_ref[:, here], far_ref[:, here].astype(F32)
        below = jnp.where(odd, chip, far)
        above = jnp.where(odd, far, chip)
        sign = stacked(sign_ref[0, :, here], sign_ref[1, :, here]).astype(F32)
        speed = stacked(speed_ref[:, here], speed_ref[:, here])
        crowd = density_ref[:, here]
        density = stacked(crowd, crowd)
        row = lax.broadcasted_iota(jnp.int32, (8, size), 0)
        in_group = row % 4
        roll = functools.partial(pltpu.roll, axis=0)
        pairs = []
        for k in range(1, 5):
            if k == 4:
                pairs.append((below, above))
            else:
                before = jnp.where(in_group < 4 - k, own, below)
                before = jnp.where(in_group >= k, roll(before, k), roll(before, 4 + k))
                after = jnp.where(in_group >= k, own, above)
                after = jnp.where(in_group < 4 - k, roll(after, 8 - k), roll(after, 4 - k))
                pairs.append((before, after))
        physics = own - upwind_change(own, pairs, sign, speed) + TIME_STEP * density
        physics = by_row(physics, row)
        crowd = jnp.where(row >= 4, density, 0.0)
        up_2, up_4, up_6 = roll(physics, 2), roll(physics, 4), roll(physics, 6)
        own_rows_ref[:, here] = jnp.where(low, physics, up_4)[0:4]
        window = jnp.where(row < 6, jnp.where(low, physics, up_6), 0.0)
        window_crowd = jnp.where(low, crowd, roll(crowd, 7))
        inner_ref[:, here] = jnp.concatenate([window, window_crowd], axis=0).astype(BF16)
        flipped = jnp.where(low, up_2, jnp.where(row < 4, up_4, physics))
        flipped_crowd = jnp.where(low, crowd, jnp.where(row == 4, roll(crowd, 5), roll(crowd, 7)))
        outer_ref[:, here] = jnp.concatenate([flipped, flipped_crowd], axis=0).astype(BF16)
        given = jnp.where(low, up_6, physics).astype(BF16)
        for j in range(3):
            swap_ref[j, :, here] = given[2 * j : 2 * j + 2]
        edge = jnp.where(low, up_2, physics)
        edge_crowd = jnp.where(low, roll(crowd, 3), roll(crowd, 6))
        edge = jnp.where(row < 2, edge, jnp.where(row == 2, edge_crowd, 0.0))
        edge_ref[:, here] = edge[0:4].astype(BF16)
        cross_ref[:, here] = jnp.where(low, physics, up_2)[0:2].astype(BF16)

    steps(own_ref.shape[1], size, body)


def correct_chunk(size, start, last, features, mix_ref, fix_ref, gain_ref, up_ref, down_ref):
    value = features[:, pl.ds(start, size + 2 * HALO)]
    patches = jnp.concatenate(
        [value[:, HALO + k : HALO + k + size] for k in range(-2, 3)], axis=0
    )
    mixed = jnp.dot(
        mix_ref[...], jnp.concatenate([patches, patches], axis=0), preferred_element_type=F32
    )
    lane = lax.broadcasted_iota(jnp.int32, (16, HALO), 1)

    def at_rim(side, keep, columns):
        column = jnp.where(keep, columns.astype(F32), 0.0).astype(BF16)
        return jnp.dot(
            fix_ref[side], jnp.concatenate([column, column], axis=0), preferred_element_type=F32
        )

    first = jnp.logical_and(lane == 0, start == 0)
    final = jnp.logical_and(lane == HALO - 1, start == last)
    head = mixed[:128, :HALO] - at_rim(0, first, value[:, HALO : 2 * HALO])
    tail = mixed[:128, size - HALO :] - at_rim(1, final, value[:, size : size + HALO])
    mixed_rows = jnp.concatenate([head, mixed[:128, HALO : size - HALO], tail], axis=1)
    square = jnp.sum(mixed_rows * mixed_rows, axis=0, keepdims=True)
    inverse = lax.rsqrt(square * (1.0 / 128.0) + EPSILON)
    normed = (mixed_rows * inverse * gain_ref[...]).astype(BF16)
    lift = jnp.dot(up_ref[...], normed, preferred_element_type=F32)
    lifted = lift + lift * jnp.tanh(lift * (GELU_0 + GELU_1 * (lift * lift)))
    result = jnp.dot(down_ref[...], lifted.astype(BF16), preferred_element_type=F32)
    return mixed[128:132] + (result[0:4] + result[4:8])


def in_groups(low, own, other):
    other = other.astype(F32)
    return jnp.where(
        low, jnp.concatenate([own, other], axis=0), jnp.concatenate([other, own], axis=0)
    )


def clear_rims(features, length):
    features[:, :HALO] = jnp.zeros((16, HALO), BF16)
    features[:, HALO + length :] = jnp.zeros((16, HALO), BF16)


def correct_inner(
    size, inner_ref, swap_ref, own_rows_ref, mix_ref, fix_ref, gain_ref, up_ref, down_ref, out_ref, features
):
    length = inner_ref.shape[1]
    low = lax.axis_index("section") == 0
    mid = slice(HALO, HALO + length)
    clear_rims(features, length)
    features[:, mid] = inner_ref[...]
    for j in range(3):
        features[6 + 2 * j : 8 + 2 * j, mid] = swap_ref[j]

    def body(start):
        here = pl.ds(start, size)
        change = correct_chunk(
            size, start, length - size, features, mix_ref, fix_ref, gain_ref, up_ref, down_ref
        )
        own = jnp.where(low, own_rows_ref[2:4, here], own_rows_ref[0:2, here])
        out_ref[:, here] = change + in_groups(low, own, swap_ref[1, :, here])

    steps(length, size, body)


def correct_outer(
    size,
    outer_ref,
    swap_ref,
    edge_ref,
    cross_ref,
    own_rows_ref,
    row_ref,
    mix_ref,
    fix_ref,
    gain_ref,
    up_ref,
    down_ref,
    out_ref,
    features,
):
    length = outer_ref.shape[1]
    low = lax.axis_index("section") == 0
    mid = slice(HALO, HALO + length)
    clear_rims(features, length)
    features[:, mid] = outer_ref[...]
    features[0:2, mid] = edge_ref[0:2]
    features[14:16, mid] = edge_ref[2:4]
    features[6:8, mid] = cross_ref[...]
    features[10:12, mid] = swap_ref[1]

    @pl.when(low)
    def _():
        features[8:10, mid] = swap_ref[0]

    @pl.when(jnp.logical_not(low))
    def _():
        features[8:10, mid] = swap_ref[2]

    def body(start):
        here = pl.ds(start, size)
        change = correct_chunk(
            size, start, length - size, features, mix_ref, fix_ref, gain_ref, up_ref, down_ref
        )
        own = jnp.where(low, own_rows_ref[0:2, here], own_rows_ref[2:4, here])
        other = jnp.where(
            low, swap_ref[0, :, here].astype(F32), swap_ref[2, :, here].astype(F32)
        )
        outer_row = change + in_groups(low, own, other)
        inner_row = row_ref[:, here]
        out_ref[:, 0, here] = jnp.where(low, outer_row, inner_row)
        out_ref[:, 1, here] = jnp.where(low, inner_row, outer_row)

    steps(length, size, body)


def halves(value):
    high = lax.reduce_precision(value, 8, 7)
    return high.astype(BF16), (value - high).astype(BF16)


def weights(low, stem_weight, conv_weight, norm_gain, up_weight, down_weight, out_weight):
    exact = functools.partial(jnp.dot, precision=lax.Precision.HIGHEST)
    channels = stem_weight.shape[1]
    stem = stem_weight.astype(F32).reshape(3, 3, 5, channels)
    conv = conv_weight[0].astype(F32)
    out = out_weight.astype(F32)
    groups = out.shape[1]
    mix = sum(
        jnp.pad(conv[s] * stem, ((0, 0), (s, 2 - s), (0, 0), (0, 0))) for s in range(3)
    )
    direct = jnp.pad(exact(stem.reshape(-1, channels), out), ((0, 0), (0, 8 - groups)))
    direct = jnp.pad(direct.reshape(3, 3, 5, 8), ((0, 0), (1, 1), (0, 0), (0, 0)))
    rims = [conv[0] * stem[:, 2], conv[2] * stem[:, 0]]
    whole = jnp.concatenate([mix, direct], axis=3)
    whole = jnp.concatenate(
        [whole] + [jnp.pad(rim, ((0, 0), (0, 0), (0, 8)))[:, None] for rim in rims], axis=1
    )

    def arranged(value, flip):
        if flip:
            value = jnp.where(low, value, value[::-1])
        fields, crowd = value[:, :, :4], value[:, :, 4]
        fields = fields.reshape(3, 7, 2, 2, -1)
        fields = jnp.where(low, fields, fields[:, :, ::-1])
        fields = jnp.transpose(fields, (1, 2, 0, 3, 4)).reshape(7, 12, -1)
        crowd = jnp.transpose(crowd, (1, 0, 2))
        if flip:
            crowd = jnp.concatenate([crowd[:, 1:], crowd[:, :1]], axis=1)
        rows = jnp.pad(jnp.concatenate([fields, crowd], axis=1), ((0, 0), (0, 1), (0, 0)))
        high, lower = halves(rows)
        mixing = jnp.concatenate([high[:5].reshape(80, -1), lower[:5].reshape(80, -1)], axis=0)
        rim = jnp.concatenate([high[5:], lower[5:]], axis=1)[:, :, :channels]
        return jnp.transpose(mixing), jnp.transpose(rim, (0, 2, 1))

    down = 0.5 * exact(down_weight[0].astype(F32), out)
    down = jnp.transpose(jnp.concatenate(halves(down), axis=1))
    shared = (jnp.transpose(norm_gain), jnp.transpose(up_weight[0]), down)
    return arranged(whole, False) + shared, arranged(whole, True) + shared


def shards(
    potential,
    speed_x,
    speed_y,
    density,
    sign_x,
    sign_y,
    stem_weight,
    conv_weight,
    norm_gain,
    up_weight,
    down_weight,
    out_weight,
):
    length = potential.shape[2]
    size = min(length, 1024)
    chunk = min(length, 512)
    low = lax.axis_index("section") == 0
    blocks = lax.axis_size("wide")
    shape = jax.ShapeDtypeStruct

    def swaps(first):
        pairs = [(2 * w + s, 2 * w + 2 + s) for w in range(first, blocks - 1, 2) for s in (0, 1)]
        return pairs + [(b, a) for a, b in pairs]

    swept, narrow = pl.pallas_call(
        functools.partial(sweep_x, size),
        out_shape=(shape((8, length), F32), shape((8, length), BF16)),
        scratch_shapes=[
            pltpu.VMEM((8, length + 2 * HALO), F32),
        ],
        name="sweep_x",
    )(potential, speed_x, sign_x)
    far = lax.ppermute(narrow, BOTH, swaps(1))
    chip = lax.ppermute(swept, BOTH, swaps(0))
    own_rows, inner, outer, given, edge, cross = pl.pallas_call(
        functools.partial(sweep_y, size),
        out_shape=(
            shape((4, length), F32),
            shape((16, length), BF16),
            shape((16, length), BF16),
            shape((3, 2, length), BF16),
            shape((4, length), BF16),
            shape((2, length), BF16),
        ),
        name="sweep_y",
    )(swept, chip, far, speed_y, sign_y, density)
    swap = lax.ppermute(given, "section", [(0, 1), (1, 0)])
    edge = lax.ppermute(
        edge,
        BOTH,
        [(2 * w + 1, 2 * w - 1) for w in range(1, blocks)]
        + [(2 * w, 2 * w + 2) for w in range(blocks - 1)],
    )
    cross = lax.ppermute(
        cross,
        BOTH,
        [(2 * w, 2 * w - 1) for w in range(1, blocks)]
        + [(2 * w + 1, 2 * w + 2) for w in range(blocks - 1)],
    )
    inner_weights, outer_weights = weights(
        low, stem_weight, conv_weight, norm_gain, up_weight, down_weight, out_weight
    )
    scratch = [pltpu.VMEM((16, length + 2 * HALO), BF16)]
    row = pl.pallas_call(
        functools.partial(correct_inner, chunk),
        out_shape=shape((4, length), F32),
        scratch_shapes=scratch,
        name="correct_inner",
    )(inner, swap, own_rows, *inner_weights)
    return pl.pallas_call(
        functools.partial(correct_outer, chunk),
        out_shape=shape((4, 2, length), F32),
        scratch_shapes=scratch,
        name="correct_outer",
    )(outer, swap, edge, cross, own_rows, row, *outer_weights)


def solution(mesh):
    placed = (
        P("section", "wide", None),
        P("wide", None),
        P("wide", None),
        P("wide", None),
        P("section", "wide", None),
        P("section", "wide", None),
        P(),
        P(),
        P(),
        P(),
        P(),
        P(),
    )
    return jax.shard_map(
        shards,
        mesh=mesh,
        in_specs=placed,
        out_specs=P(None, ("wide", "section"), None),
        check_vma=False,
    )
```

time: 375 us -> 106 us (0.28)
  the two profiles are of different devices: /device:TPU:32 before, /device:TPU:7 now
where the time goes in v1:
time: 106 us
  Pallas kernels  68.3 us (64%)
  starting transfers between devices  24.7 us (23%)
  local copies, waits for them, and re-layouts  9.49 us (9%)
  other arithmetic  2.3 us (2%)
    pallas_call x1, Pallas kernels, shards(): pl.pallas_call(functools.partial(correct_outer, chunk), out_shape=shape((...  28.1 us
    pallas_call x1, Pallas kernels, shards(): pl.pallas_call(functools.partial(correct_inner, chunk), out_shape=shape((...  27.5 us
    ppermute x1, starting transfers between devices, shards(): lax.ppermute(cross, BOTH, [(2 * w, 2 * w - 1) for w in range(1, blocks)]...  11.2 us
    pallas_call x1, Pallas kernels, shards(): pl.pallas_call(functools.partial(sweep_x, size), out_shape=(shape((8, len...  7.88 us
    unnamed x29, local copies, waits for them, and re-layouts  7.08 us
    ppermute x1, starting transfers between devices, shards(): swap = lax.ppermute(given, 'section', [(0, 1), (1, 0)])  6.71 us
    pallas_call x1, Pallas kernels, shards(): pl.pallas_call(functools.partial(sweep_y, size), out_shape=(shape((4, len...  4.85 us
    ppermute x1, starting transfers between devices, shards(): far = lax.ppermute(narrow, BOTH, swaps(1))  3.55 us
  transfers between devices with their start and end apart: 5, of which 1 were waited for; matrix products, arithmetic and copies ran while one was open for 6% of the time, Pallas kernels for 26%

profile of v1, /device:TPU:7, one launch (start us, length us, event | category | flops | bytes accessed | tf_op | source)
XLA Modules:
  0.0 105.6 jit_solution(13229949805361395001)
XLA Ops:
  0.0 0.0 copy-start
  0.0 7.9 %sweep_x.1 = (f32[8,16384]{1,0:T(8,128)}, bf16[8,16384]{1,0:T(8,128)(2,1)}) custom-call(f32[2,4,16384]{2,1,0:T(4,128)} %pot_ref.1, f32[4,16384]{1,0:T(4,128)} %speed_ref.2, s32[2,4,16384]{2,1,0:T(4,128)} %sign_ref.2), custom_call_target="tpu_custom_call" | custom-call | tf_op jit(solution)/shard_map/sweep_x/pallas_call | solution.py:325
  7.9 0.7 collective-permute-start
  8.6 3.6 %collective-permute-start.1 = (bf16[8,16384]{1,0:T(8,128)(2,1)}, bf16[8,16384]{1,0:T(8,128)(2,1)S(1)}, u32[]{:S(2)}, u32[]{:S(2)}) collective-permute-start(bf16[8,16384]{1,0:T(8,128)(2,1)} %get-tuple-element.14), channel_id=1, source_target_pairs={{2,4},{3,5},{6,8},{7,9},{10,12},{11,13},{14,16},{15,17},{18,20},{1... | collective-permute-start | bytes 786440 | tf_op jit(solution)/shard_map/ppermute | solution.py:333
  12.1 0.0 copy-done.8
  12.2 0.0 copy-done.10
  12.2 0.0 copy-start.9
  12.3 0.6 copy-done.9
  12.9 0.1 fusion.8
  13.0 0.1 reshape.47
  13.1 0.1 copy.85
  13.4 0.1 pad_maximum_fusion
  13.8 0.0 copy-start.3
  13.8 0.6 copy-done.3
  14.4 0.1 copy.94
  14.5 0.1 copy.93
  14.7 0.6 slice-done
  15.5 0.1 copy.104
  15.7 0.1 copy.103
  15.8 0.7 maximum_bitcast_fusion.mix_ref
  16.5 0.7 maximum_bitcast_fusion.1.mix_ref
  17.2 0.1 reduce-precision_convert_fusion.2
  17.4 0.1 collective-permute-done.1.far_ref
  17.5 0.0 collective-permute-done.chip_ref
  17.5 0.7 copy-done.4
  18.1 0.8 copy-done.2
  18.9 4.9 %sweep_y.1 = (f32[4,16384]{1,0:T(4,128)}, bf16[16,16384]{1,0:T(8,128)(2,1)}, bf16[16,16384]{1,0:T(8,128)(2,1)}, bf16[3,2,16384]{2,1,0:T(2,128)(2,1)}, bf16[4,163...) custom-call(f32[8,16384]{1,0:T(8,128)} %get-tuple-element.13.own_ref, f32[8,16384]{1,0:T(8,128)} %copy-done.2, ...), custom_call_target="tpu_custom_call" | custom-call | tf_op jit(solution)/shard_map/sweep_y/pallas_call | solution.py:335
  23.8 6.7 %collective-permute-start.2 = (bf16[3,2,16384]{2,1,0:T(2,128)(2,1)}, bf16[3,2,16384]{2,1,0:T(2,128)(2,1)S(1)}, u32[]{:S(2)}, u32[]{:S(2)}) collective-permute-start(bf16[3,2,16384]{2,1,0:T(2,128)(2,1)} %get-tuple-element.16), channel_id=1, source_target_pairs={{0,1},{1,0},{2,3},{3,2},{4,5},{5,4},{6,7},{7,6},{8,9},{9,8},{10,11... | collective-permute-start | bytes 589832 | tf_op jit(solution)/shard_map/ppermute | solution.py:347
  30.5 2.5 %collective-permute-start.3 = (bf16[4,16384]{1,0:T(4,128)(2,1)}, bf16[4,16384]{1,0:T(4,128)(2,1)S(1)}, u32[]{:S(2)}, u32[]{:S(2)}) collective-permute-start(bf16[4,16384]{1,0:T(4,128)(2,1)} %get-tuple-element.17), channel_id=1, source_target_pairs={{3,1},{5,3},{7,5},{9,7},{11,9},{13,11},{15,13},{17,15},{19,17},{21... | collective-permute-start | bytes 393224 | tf_op jit(solution)/shard_map/ppermute | solution.py:348
  33.0 0.0 copy-start.7
  33.0 0.7 copy.109
  33.8 0.7 copy-done.11
  34.4 0.7 copy.97.gain_ref
  35.2 0.0 copy-done.7
  35.2 0.7 copy.96
  35.9 0.7 copy.110
  36.6 0.1 copy-done.12
  36.8 11.2 %collective-permute-start.4 = (bf16[2,16384]{1,0:T(2,128)(2,1)S(1)}, bf16[2,16384]{1,0:T(2,128)(2,1)S(1)}, u32[]{:S(2)}, u32[]{:S(2)}) collective-permute-start(bf16[2,16384]{1,0:T(2,128)(2,1)S(1)} %copy-done.12), channel_id=1, source_target_pairs={{2,1},{4,3},{6,5},{8,7},{10,9},{12,11},{14,13},{16,15},{18,17},{20... | collective-permute-start | bytes 196616 | tf_op jit(solution)/shard_map/ppermute | solution.py:354
  48.0 0.6 maximum_bitcast_fusion.2.down_ref
  48.6 0.0 collective-permute-done.2.swap_ref
  48.6 0.7 copy-done.1
  49.2 27.5 %correct_inner.1.row_ref = f32[4,16384]{1,0:T(4,128)} custom-call(bf16[16,16384]{1,0:T(8,128)(2,1)} %get-tuple-element.20.inner_ref, bf16[3,2,16384]{2,1,0:T(2,128)(2,1)} %copy-done.1, f32[4,16384]{1,0:T(4,128)} %get-tuple-element.19.own_rows_ref, bf16[136,160]{1,0:T(8,128)(2,1)} %maximum_bitcast_fusion.mix_ref, bf16[2,128,32]{2,1,0:T(8,128)(2,1)} %bitcast.67, ...), custom_call_target="tpu_custom_call" | custom-call | tf_op jit(solution)/shard_map/correct_inner/pallas_call | solution.py:364
  76.7 0.0 collective-permute-done.4.cross_ref
  76.7 0.0 collective-permute-done.3.edge_ref
  76.7 0.0 copy-start.5
  76.7 0.6 copy-done.6
  77.3 0.1 copy-done.5
  77.4 28.1 %correct_outer.1 = f32[4,2,16384]{2,1,0:T(2,128)} custom-call(bf16[16,16384]{1,0:T(8,128)(2,1)} %get-tuple-element.15.outer_ref, bf16[3,2,16384]{2,1,0:T(2,128)(2,1)} %copy-done.1, bf16[4,16384]{1,0:T(4,128)(2,1)} %copy-done.5, bf16[2,16384]{1,0:T(2,128)(2,1)} %copy-done.6, f32[4,16384]{1,0:T(4,128)} %get-tuple-element.19.own_rows_ref, ...), custom_call_target="tpu_custom_call" | custom-call | tf_op jit(solution)/shard_map/correct_outer/pallas_call | solution.py:370
  (51 shorter events, 0.6 us)
Async XLA Ops:
  0.0 17.2 %copy-start = (bf16[1,256,128]{2,1,0:T(8,128)(2,1)S(1)}, bf16[1,256,128]{2,1,0:T(8,128)(2,1)}, u32[]{:S(2)}) copy-start(bf16[1,256,128]{2,1,0:T(8,128)(2,1)} %param.22) | copy-start | bytes 196612
  0.0 12.1 %copy-start.8 = (bf16[45,128]{1,0:T(8,128)(2,1)S(1)}, bf16[45,128]{1,0:T(8,128)(2,1)}, u32[]{:S(2)}) copy-start(bf16[45,128]{1,0:T(8,128)(2,1)} %param.18) | copy-start | bytes 34564
  7.9 9.6 %collective-permute-start = (f32[8,16384]{1,0:T(8,128)}, f32[8,16384]{1,0:T(8,128)S(1)}, u32[]{:S(2)}, u32[]{:S(2)}) collective-permute-start(f32[8,16384]{1,0:T(8,128)} %get-tuple-element.13.own_ref), channel_id=1, source_target_pairs={{0,2},{1,3},{4,6},{5,7},{8,10},{9,11},{12,14},{13,15},{16,18},{17,... | collective-permute-start | bytes 1572872 | tf_op jit(solution)/shard_map/ppermute | solution.py:334
  8.6 3.6 %copy-start.10 = (bf16[1,3,128]{2,1,0:T(4,128)(2,1)S(1)}, bf16[1,3,128]{2,1,0:T(4,128)(2,1)}, u32[]{:S(2)}) copy-start(bf16[1,3,128]{2,1,0:T(4,128)(2,1)} %param.19) | copy-start | bytes 2308
  8.6 8.9 %collective-permute-start.1 = (bf16[8,16384]{1,0:T(8,128)(2,1)}, bf16[8,16384]{1,0:T(8,128)(2,1)S(1)}, u32[]{:S(2)}, u32[]{:S(2)}) collective-permute-start(bf16[8,16384]{1,0:T(8,128)(2,1)} %get-tuple-element.14), channel_id=1, source_target_pairs={{2,4},{3,5},{6,8},{7,9},{10,12},{11,13},{14,16},{15,17},{18,20},{1... | collective-permute-start | bytes 786440 | tf_op jit(solution)/shard_map/ppermute | solution.py:333
  12.2 0.7 copy-start.9
  13.8 0.7 copy-start.3
  14.4 0.9 slice-start
  17.5 0.7 copy-start.4
  18.1 0.8 copy-start.2
  23.8 24.8 %collective-permute-start.2 = (bf16[3,2,16384]{2,1,0:T(2,128)(2,1)}, bf16[3,2,16384]{2,1,0:T(2,128)(2,1)S(1)}, u32[]{:S(2)}, u32[]{:S(2)}) collective-permute-start(bf16[3,2,16384]{2,1,0:T(2,128)(2,1)} %get-tuple-element.16), channel_id=1, source_target_pairs={{0,1},{1,0},{2,3},{3,2},{4,5},{5,4},{6,7},{7,6},{8,9},{9,8},{10,11... | collective-permute-start | bytes 589832 | tf_op jit(solution)/shard_map/ppermute | solution.py:347
  30.5 46.2 %collective-permute-start.3 = (bf16[4,16384]{1,0:T(4,128)(2,1)}, bf16[4,16384]{1,0:T(4,128)(2,1)S(1)}, u32[]{:S(2)}, u32[]{:S(2)}) collective-permute-start(bf16[4,16384]{1,0:T(4,128)(2,1)} %get-tuple-element.17), channel_id=1, source_target_pairs={{3,1},{5,3},{7,5},{9,7},{11,9},{13,11},{15,13},{17,15},{19,17},{21... | collective-permute-start | bytes 393224 | tf_op jit(solution)/shard_map/ppermute | solution.py:348
  33.0 2.1 %copy-start.7 = (bf16[1,128,256]{2,1,0:T(8,128)(2,1)S(1)}, bf16[1,128,256]{2,1,0:T(8,128)(2,1)}, u32[]{:S(2)}) copy-start(bf16[1,128,256]{2,1,0:T(8,128)(2,1)} %param.21) | copy-start | bytes 196612
  33.8 0.7 copy-start.11
  35.9 0.8 copy-start.12
  36.8 40.0 %collective-permute-start.4 = (bf16[2,16384]{1,0:T(2,128)(2,1)S(1)}, bf16[2,16384]{1,0:T(2,128)(2,1)S(1)}, u32[]{:S(2)}, u32[]{:S(2)}) collective-permute-start(bf16[2,16384]{1,0:T(2,128)(2,1)S(1)} %copy-done.12), channel_id=1, source_target_pairs={{2,1},{4,3},{6,5},{8,7},{10,9},{12,11},{14,13},{16,15},{18,17},{20... | collective-permute-start | bytes 196616 | tf_op jit(solution)/shard_map/ppermute | solution.py:354
  48.6 0.7 copy-start.1
  76.7 0.6 copy-start.6
  76.7 0.7 copy-start.5

commit v2 on v1

--- a/solution.py
+++ b/solution.py
@@ -2,6 +2,7 @@
 
 import jax
 import jax.numpy as jnp
+import numpy as np
 from jax import lax
 from jax.experimental import pallas as pl
 from jax.experimental.pallas import tpu as pltpu
@@ -18,6 +19,7 @@
 F32 = jnp.float32
 BOTH = ("wide", "section")
 HALO = 128
+LAG = 2
 
 
 def steps(length, size, body):
@@ -137,34 +139,61 @@
     steps(own_ref.shape[1], size, body)
 
 
-def correct_chunk(size, start, last, features, mix_ref, fix_ref, gain_ref, up_ref, down_ref):
-    value = features[:, pl.ds(start, size + 2 * HALO)]
+def mix_features(size, start, length, features, mix_ref, fix_ref):
+    value = features[:, start : start + size + 2 * HALO]
     patches = jnp.concatenate(
         [value[:, HALO + k : HALO + k + size] for k in range(-2, 3)], axis=0
     )
-    mixed = jnp.dot(
-        mix_ref[...], jnp.concatenate([patches, patches], axis=0), preferred_element_type=F32
-    )
+    mixed = jnp.dot(mix_ref[...], patches, preferred_element_type=F32)
+    change = mixed[128:132] + mixed[132:136]
+    mixed = mixed[:128]
     lane = lax.broadcasted_iota(jnp.int32, (16, HALO), 1)
 
-    def at_rim(side, keep, columns):
-        column = jnp.where(keep, columns.astype(F32), 0.0).astype(BF16)
-        return jnp.dot(
-            fix_ref[side], jnp.concatenate([column, column], axis=0), preferred_element_type=F32
-        )
-
-    first = jnp.logical_and(lane == 0, start == 0)
-    final = jnp.logical_and(lane == HALO - 1, start == last)
-    head = mixed[:128, :HALO] - at_rim(0, first, value[:, HALO : 2 * HALO])
-    tail = mixed[:128, size - HALO :] - at_rim(1, final, value[:, size : size + HALO])
-    mixed_rows = jnp.concatenate([head, mixed[:128, HALO : size - HALO], tail], axis=1)
-    square = jnp.sum(mixed_rows * mixed_rows, axis=0, keepdims=True)
+    def at_rim(side, place, columns):
+        column = jnp.where(lane == place, columns.astype(F32), 0.0).astype(BF16)
+        return jnp.dot(fix_ref[side], column, preferred_element_type=F32)
+
+    if start == 0:
+        head = mixed[:, :HALO] - at_rim(0, 0, value[:, HALO : 2 * HALO])
+        mixed = jnp.concatenate([head, mixed[:, HALO:]], axis=1)
+    if start + size == length:
+        tail = mixed[:, size - HALO :] - at_rim(1, HALO - 1, value[:, size : size + HALO])
+        mixed = jnp.concatenate([mixed[:, : size - HALO], tail], axis=1)
+    return mixed, change
+
+
+def normalise(mixed, gain):
+    square = jnp.sum(mixed * mixed, axis=0, keepdims=True)
     inverse = lax.rsqrt(square * (1.0 / 128.0) + EPSILON)
-    normed = (mixed_rows * inverse * gain_ref[...]).astype(BF16)
-    lift = jnp.dot(up_ref[...], normed, preferred_element_type=F32)
-    lifted = lift + lift * jnp.tanh(lift * (GELU_0 + GELU_1 * (lift * lift)))
-    result = jnp.dot(down_ref[...], lifted.astype(BF16), preferred_element_type=F32)
-    return mixed[128:132] + (result[0:4] + result[4:8])
+    return (mixed * inverse * gain).astype(BF16)
+
+
+def lift_twice(normed, up_ref):
+    lift = jnp.dot(up_ref[...], normed, preferred_element_type=F32).astype(BF16)
+    inner = BF16(GELU_0) + BF16(GELU_1) * (lift * lift)
+    return lift + lift * jnp.tanh(lift * inner)
+
+
+def correct(size, length, features, weight_refs, finish):
+    mix_ref, fix_ref, gain_ref, up_ref, down_ref = weight_refs
+    gain = jnp.broadcast_to(gain_ref[...], (128, size))
+    count = length // size
+    mixed, normed, lifted, changes = {}, {}, {}, {}
+    for t in range(count + 3 * LAG):
+        if t < count:
+            mixed[t], changes[t] = mix_features(
+                size, t * size, length, features, mix_ref, fix_ref
+            )
+        u = t - 3 * LAG
+        if u >= 0:
+            result = jnp.dot(down_ref[...], lifted.pop(u), preferred_element_type=F32)
+            finish(slice(u * size, u * size + size), changes.pop(u) + (result[0:4] + result[4:8]))
+        u = t - 2 * LAG
+        if 0 <= u < count:
+            lifted[u] = lift_twice(normed.pop(u), up_ref)
+        u = t - LAG
+        if 0 <= u < count:
+            normed[u] = normalise(mixed.pop(u), gain)
 
 
 def in_groups(low, own, other):
@@ -179,9 +208,8 @@
     features[:, HALO + length :] = jnp.zeros((16, HALO), BF16)
 
 
-def correct_inner(
-    size, inner_ref, swap_ref, own_rows_ref, mix_ref, fix_ref, gain_ref, up_ref, down_ref, out_ref, features
-):
+def correct_inner(size, inner_ref, swap_ref, own_rows_ref, *refs):
+    *weight_refs, out_ref, features = refs
     length = inner_ref.shape[1]
     low = lax.axis_index("section") == 0
     mid = slice(HALO, HALO + length)
@@ -190,33 +218,17 @@
     for j in range(3):
         features[6 + 2 * j : 8 + 2 * j, mid] = swap_ref[j]
 
-    def body(start):
-        here = pl.ds(start, size)
-        change = correct_chunk(
-            size, start, length - size, features, mix_ref, fix_ref, gain_ref, up_ref, down_ref
-        )
+    def finish(here, change):
         own = jnp.where(low, own_rows_ref[2:4, here], own_rows_ref[0:2, here])
         out_ref[:, here] = change + in_groups(low, own, swap_ref[1, :, here])
 
-    steps(length, size, body)
+    correct(size, length, features, weight_refs, finish)
 
 
 def correct_outer(
-    size,
-    outer_ref,
-    swap_ref,
-    edge_ref,
-    cross_ref,
-    own_rows_ref,
-    row_ref,
-    mix_ref,
-    fix_ref,
-    gain_ref,
-    up_ref,
-    down_ref,
-    out_ref,
-    features,
+    size, outer_ref, swap_ref, edge_ref, cross_ref, own_rows_ref, row_ref, *refs
 ):
+    *weight_refs, out_ref, features = refs
     length = outer_ref.shape[1]
     low = lax.axis_index("section") == 0
     mid = slice(HALO, HALO + length)
@@ -235,11 +247,7 @@
     def _():
         features[8:10, mid] = swap_ref[2]
 
-    def body(start):
-        here = pl.ds(start, size)
-        change = correct_chunk(
-            size, start, length - size, features, mix_ref, fix_ref, gain_ref, up_ref, down_ref
-        )
+    def finish(here, change):
         own = jnp.where(low, own_rows_ref[0:2, here], own_rows_ref[2:4, here])
         other = jnp.where(
             low, swap_ref[0, :, here].astype(F32), swap_ref[2, :, here].astype(F32)
@@ -249,52 +257,65 @@
         out_ref[:, 0, here] = jnp.where(low, outer_row, inner_row)
         out_ref[:, 1, here] = jnp.where(low, inner_row, outer_row)
 
-    steps(length, size, body)
-
-
-def halves(value):
-    high = lax.reduce_precision(value, 8, 7)
-    return high.astype(BF16), (value - high).astype(BF16)
-
-
-def weights(low, stem_weight, conv_weight, norm_gain, up_weight, down_weight, out_weight):
-    exact = functools.partial(jnp.dot, precision=lax.Precision.HIGHEST)
-    channels = stem_weight.shape[1]
-    stem = stem_weight.astype(F32).reshape(3, 3, 5, channels)
-    conv = conv_weight[0].astype(F32)
-    out = out_weight.astype(F32)
-    groups = out.shape[1]
-    mix = sum(
-        jnp.pad(conv[s] * stem, ((0, 0), (s, 2 - s), (0, 0), (0, 0))) for s in range(3)
-    )
-    direct = jnp.pad(exact(stem.reshape(-1, channels), out), ((0, 0), (0, 8 - groups)))
-    direct = jnp.pad(direct.reshape(3, 3, 5, 8), ((0, 0), (1, 1), (0, 0), (0, 0)))
-    rims = [conv[0] * stem[:, 2], conv[2] * stem[:, 0]]
-    whole = jnp.concatenate([mix, direct], axis=3)
-    whole = jnp.concatenate(
-        [whole] + [jnp.pad(rim, ((0, 0), (0, 0), (0, 8)))[:, None] for rim in rims], axis=1
-    )
-
-    def arranged(value, flip):
-        if flip:
-            value = jnp.where(low, value, value[::-1])
-        fields, crowd = value[:, :, :4], value[:, :, 4]
-        fields = fields.reshape(3, 7, 2, 2, -1)
-        fields = jnp.where(low, fields, fields[:, :, ::-1])
-        fields = jnp.transpose(fields, (1, 2, 0, 3, 4)).reshape(7, 12, -1)
-        crowd = jnp.transpose(crowd, (1, 0, 2))
-        if flip:
-            crowd = jnp.concatenate([crowd[:, 1:], crowd[:, :1]], axis=1)
-        rows = jnp.pad(jnp.concatenate([fields, crowd], axis=1), ((0, 0), (0, 1), (0, 0)))
-        high, lower = halves(rows)
-        mixing = jnp.concatenate([high[:5].reshape(80, -1), lower[:5].reshape(80, -1)], axis=0)
-        rim = jnp.concatenate([high[5:], lower[5:]], axis=1)[:, :, :channels]
-        return jnp.transpose(mixing), jnp.transpose(rim, (0, 2, 1))
-
-    down = 0.5 * exact(down_weight[0].astype(F32), out)
-    down = jnp.transpose(jnp.concatenate(halves(down), axis=1))
-    shared = (jnp.transpose(norm_gain), jnp.transpose(up_weight[0]), down)
-    return arranged(whole, False) + shared, arranged(whole, True) + shared
+    correct(size, length, features, weight_refs, finish)
+
+
+def selections():
+    picks = np.zeros((2, 2, 6, 45, 128), np.float32)
+    for section in range(2):
+        for outer in range(2):
+            places = []
+            for row in range(3):
+                for group in range(4):
+                    other = int(group // 2 != section)
+                    shift = 2 - row if outer and section else row
+                    places.append((6 * other + 2 * row + group % 2, shift, group))
+                crowd = 12 + ((row + 2) % 3 if outer else row)
+                places.append((crowd, shift, 4))
+            for place, shift, channel in places:
+                for column in range(3):
+                    source = 15 * shift + 5 * column + channel
+                    for tap in range(3):
+                        picks[section, outer, tap, source, 16 * (tap + column) + place] = 1.0
+                    picks[section, outer, 3, source, 16 * (column + 1) + place] = 1.0
+                picks[section, outer, 4, 15 * shift + 10 + channel, place] = 1.0
+                picks[section, outer, 5, 15 * shift + channel, place] = 1.0
+    return picks.transpose(0, 1, 3, 2, 4).reshape(2, 2, 45, 768)
+
+
+def prepare(pick_ref, stem_ref, conv_ref, gain_ref, up_ref, down_ref, out_ref, *refs):
+    inner_refs, outer_refs, (gain_out, up_out, down_out) = refs[0:2], refs[2:4], refs[4:7]
+    section = lax.axis_index("section")
+
+    def turned(left, right):
+        return lax.dot_general(
+            left, right, (((0,), (0,)), ((), ())), preferred_element_type=F32
+        )
+
+    def unit(size):
+        rows = lax.broadcasted_iota(jnp.int32, (size, size), 0)
+        return jnp.where(rows == lax.broadcasted_iota(jnp.int32, (size, size), 1), 1.0, 0.0)
+
+    def split(value):
+        high = value.astype(BF16)
+        return high, (value - high.astype(F32)).astype(BF16)
+
+    conv = turned(conv_ref[0], unit(3).astype(BF16))
+    for outer, (mix_out, fix_out) in enumerate((inner_refs, outer_refs)):
+        picked = turned(stem_ref[...], pick_ref[section, outer])
+        parts = [picked[:, 128 * i : 128 * i + 128] for i in range(6)]
+        mix = sum(conv[:, i : i + 1] * parts[i] for i in range(3))
+        direct = turned(out_ref[...], parts[3].astype(BF16))
+        rows = jnp.concatenate([mix, direct, direct - direct.astype(BF16).astype(F32)], axis=0)
+        mix_out[...] = rows[:, :80].astype(BF16)
+        fix_out[0] = (conv[:, 0:1] * parts[4])[:, :16].astype(BF16)
+        fix_out[1] = (conv[:, 2:3] * parts[5])[:, :16].astype(BF16)
+    gain_out[...] = jnp.sum(unit(128) * gain_ref[...], axis=1, keepdims=True)
+    up_out[...] = turned(up_ref[0], unit(128).astype(BF16)).astype(BF16)
+    down = 0.5 * lax.dot_general(
+        out_ref[...], down_ref[0], (((0,), (1,)), ((), ())), preferred_element_type=F32
+    )
+    down_out[...] = jnp.concatenate([down, down - down.astype(BF16).astype(F32)], axis=0).astype(BF16)
 
 
 def shards(
@@ -312,9 +333,8 @@
     out_weight,
 ):
     length = potential.shape[2]
-    size = min(length, 1024)
+    size = min(length, 4096)
     chunk = min(length, 512)
-    low = lax.axis_index("section") == 0
     blocks = lax.axis_size("wide")
     shape = jax.ShapeDtypeStruct
 
@@ -357,9 +377,20 @@
         [(2 * w, 2 * w - 1) for w in range(1, blocks)]
         + [(2 * w + 1, 2 * w + 2) for w in range(blocks - 1)],
     )
-    inner_weights, outer_weights = weights(
-        low, stem_weight, conv_weight, norm_gain, up_weight, down_weight, out_weight
-    )
+    mix_shapes = (shape((136, 80), BF16), shape((2, 128, 16), BF16))
+    shared_shapes = (shape((128, 1), F32), shape((256, 128), BF16), shape((8, 256), BF16))
+    made = pl.pallas_call(
+        prepare, out_shape=mix_shapes + mix_shapes + shared_shapes, name="prepare"
+    )(
+        jnp.asarray(selections(), BF16),
+        stem_weight,
+        conv_weight,
+        norm_gain,
+        up_weight,
+        down_weight,
+        out_weight,
+    )
+    inner_weights, outer_weights = made[0:2] + made[4:7], made[2:7]
     scratch = [pltpu.VMEM((16, length + 2 * HALO), BF16)]
     row = pl.pallas_call(
         functools.partial(correct_inner, chunk),

time: 106 us -> 63 us (0.59)
  Pallas kernels: 68.3 us -> 29.1 us
  local copies, waits for them, and re-layouts: 9.49 us -> 3.6 us
  waiting for transfers between devices: 0.11 us -> 5.35 us
  other arithmetic: 2.3 us -> 0 us
    pallas_call x1, Pallas kernels: 28.1 us -> 8.84 us  [shards(): pl.pallas_call(functools.partial(correct_outer, chunk), out_shape=shape((...]
    pallas_call x1, Pallas kernels: 27.5 us -> 8.22 us  [shards(): pl.pallas_call(functools.partial(correct_inner, chunk), out_shape=shape((...]
    ppermute x1, waiting for transfers between devices: 0.1 us -> 5.34 us  [shards(): far = lax.ppermute(narrow, BOTH, swaps(1))]
    unnamed x29 -> x13, local copies, waits for them, and re-layouts: 7.08 us -> 3.6 us
    pallas_call x1, Pallas kernels: 7.88 us -> 5.28 us  [shards(): pl.pallas_call(functools.partial(sweep_x, size), out_shape=(shape((8, len...]
    pallas_call x0 -> x1, Pallas kernels: none -> 2.17 us  [shards(): pl.pallas_call(prepare, out_shape=mix_shapes + mix_shapes + shared_shapes...]
    transpose x5 -> x0, other arithmetic: 2.1 us -> none  [the longest x2 1.43 us: arranged(): return (jnp.transpose(mixing), jnp.transpose(rim, (0, 2, 1)))]
  transfers between devices with their start and end apart: 5 -> 5, of which waited for: 1 -> 1; matrix products, arithmetic and copies ran while one was open for 6% -> 1% of each run, Pallas kernels for 26% -> 17%
where the time goes in v2:
time: 63 us; the launch traced here: 62.8 us
  Pallas kernels  29.1 us (46%)
  starting transfers between devices  24.7 us (39%)
  waiting for transfers between devices  5.35 us (8%)
  local copies, waits for them, and re-layouts  3.6 us (6%)
    ppermute x1, starting transfers between devices, shards(): lax.ppermute(cross, BOTH, [(2 * w, 2 * w - 1) for w in range(1, blocks)]...  11.6 us
    pallas_call x1, Pallas kernels, shards(): pl.pallas_call(functools.partial(correct_outer, chunk), out_shape=shape((...  8.84 us
    pallas_call x1, Pallas kernels, shards(): pl.pallas_call(functools.partial(correct_inner, chunk), out_shape=shape((...  8.22 us
    ppermute x1, starting transfers between devices, shards(): swap = lax.ppermute(given, 'section', [(0, 1), (1, 0)])  6.71 us
    ppermute x1, waiting for transfers between devices, shards(): far = lax.ppermute(narrow, BOTH, swaps(1))  5.34 us
    pallas_call x1, Pallas kernels, shards(): pl.pallas_call(functools.partial(sweep_x, size), out_shape=(shape((8, len...  5.28 us
    pallas_call x1, Pallas kernels, shards(): pl.pallas_call(functools.partial(sweep_y, size), out_shape=(shape((4, len...  4.58 us
    unnamed x13, local copies, waits for them, and re-layouts  3.6 us
  transfers between devices with their start and end apart: 5, of which 1 were waited for; matrix products, arithmetic and copies ran while one was open for 1% of the time, Pallas kernels for 17%

profile of v2, /device:TPU:7, one launch (start us, length us, event | category | flops | bytes accessed | tf_op | source)
XLA Modules:
  0.0 62.8 jit_solution(5921107143064131493)
XLA Ops:
  0.0 5.3 %sweep_x.1 = (f32[8,16384]{1,0:T(8,128)}, bf16[8,16384]{1,0:T(8,128)(2,1)}) custom-call(f32[2,4,16384]{2,1,0:T(4,128)} %pot_ref.1, f32[4,16384]{1,0:T(4,128)} %speed_ref.2, s32[2,4,16384]{2,1,0:T(4,128)} %sign_ref.2), custom_call_target="tpu_custom_call" | custom-call | tf_op jit(solution)/shard_map/sweep_x/pallas_call | solution.py:345
  5.3 0.7 %collective-permute-start = (f32[8,16384]{1,0:T(8,128)}, f32[8,16384]{1,0:T(8,128)S(1)}, u32[]{:S(2)}, u32[]{:S(2)}) collective-permute-start(f32[8,16384]{1,0:T(8,128)} %get-tuple-element.20.own_ref), channel_id=1, source_target_pairs={{0,2},{1,3},{4,6},{5,7},{8,10},{9,11},{12,14},{13,15},{16,18},{17,... | collective-permute-start | bytes 1572872 | tf_op jit(solution)/shard_map/ppermute | solution.py:354
  6.0 3.4 %collective-permute-start.1 = (bf16[8,16384]{1,0:T(8,128)(2,1)}, bf16[8,16384]{1,0:T(8,128)(2,1)S(1)}, u32[]{:S(2)}, u32[]{:S(2)}) collective-permute-start(bf16[8,16384]{1,0:T(8,128)(2,1)} %get-tuple-element.21), channel_id=1, source_target_pairs={{2,4},{3,5},{6,8},{7,9},{10,12},{11,13},{14,16},{15,17},{18,20},{1... | collective-permute-start | bytes 786440 | tf_op jit(solution)/shard_map/ppermute | solution.py:353
  9.4 5.3 %collective-permute-done.1.far_ref = bf16[8,16384]{1,0:T(8,128)(2,1)S(1)} collective-permute-done((bf16[8,16384]{1,0:T(8,128)(2,1)}, bf16[8,16384]{1,0:T(8,128)(2,1)S(1)}, u32[]{:S(2)}, u32[]{:S(2)}) %collective-permute-start.1) | collective-permute-done | bytes 262176 | tf_op jit(solution)/shard_map/ppermute | solution.py:353
  14.7 0.0 copy-start.2
  14.7 0.0 collective-permute-done.chip_ref
  14.7 0.7 %copy-done.2 = bf16[8,16384]{1,0:T(8,128)(2,1)} copy-done((bf16[8,16384]{1,0:T(8,128)(2,1)}, bf16[8,16384]{1,0:T(8,128)(2,1)S(1)}, u32[]{:S(2)}) %copy-start.2) | copy-done | bytes 262168
  15.4 0.0 copy-start.1
  15.4 0.8 %copy-done.1 = f32[8,16384]{1,0:T(8,128)} copy-done((f32[8,16384]{1,0:T(8,128)}, f32[8,16384]{1,0:T(8,128)S(1)}, u32[]{:S(2)}) %copy-start.1) | copy-done | bytes 524312
  16.3 4.6 %sweep_y.1 = (f32[4,16384]{1,0:T(4,128)}, bf16[16,16384]{1,0:T(8,128)(2,1)}, bf16[16,16384]{1,0:T(8,128)(2,1)}, bf16[3,2,16384]{2,1,0:T(2,128)(2,1)}, bf16[4,163...) custom-call(f32[8,16384]{1,0:T(8,128)} %get-tuple-element.20.own_ref, f32[8,16384]{1,0:T(8,128)} %copy-done.1, ...), custom_call_target="tpu_custom_call" | custom-call | tf_op jit(solution)/shard_map/sweep_y/pallas_call | solution.py:355
  20.9 6.7 %collective-permute-start.2 = (bf16[3,2,16384]{2,1,0:T(2,128)(2,1)}, bf16[3,2,16384]{2,1,0:T(2,128)(2,1)S(1)}, u32[]{:S(2)}, u32[]{:S(2)}) collective-permute-start(bf16[3,2,16384]{2,1,0:T(2,128)(2,1)} %get-tuple-element.23), channel_id=1, source_target_pairs={{0,1},{1,0},{2,3},{3,2},{4,5},{5,4},{6,7},{7,6},{8,9},{9,8},{10,11... | collective-permute-start | bytes 589832 | tf_op jit(solution)/shard_map/ppermute | solution.py:367
  27.6 0.0 copy-start.5
  27.6 2.3 %collective-permute-start.3 = (bf16[4,16384]{1,0:T(4,128)(2,1)}, bf16[4,16384]{1,0:T(4,128)(2,1)S(1)}, u32[]{:S(2)}, u32[]{:S(2)}) collective-permute-start(bf16[4,16384]{1,0:T(4,128)(2,1)} %get-tuple-element.24), channel_id=1, source_target_pairs={{3,1},{5,3},{7,5},{9,7},{11,9},{13,11},{15,13},{17,15},{19,17},{21... | collective-permute-start | bytes 393224 | tf_op jit(solution)/shard_map/ppermute | solution.py:368
  29.8 11.6 %collective-permute-start.4 = (bf16[2,16384]{1,0:T(2,128)(2,1)}, bf16[2,16384]{1,0:T(2,128)(2,1)S(1)}, u32[]{:S(2)}, u32[]{:S(2)}) collective-permute-start(bf16[2,16384]{1,0:T(2,128)(2,1)} %get-tuple-element.25), channel_id=1, source_target_pairs={{2,1},{4,3},{6,5},{8,7},{10,9},{12,11},{14,13},{16,15},{18,17},{20... | collective-permute-start | bytes 196616 | tf_op jit(solution)/shard_map/ppermute | solution.py:374
  41.4 0.0 copy-done.5
  41.5 0.7 %copy.14.out_ref = bf16[128,4]{1,0:T(8,128)(2,1)} copy(bf16[128,4]{0,1:T(4,128)(2,1)S(1)} %copy-done.5) | data formatting | bytes 2048 | tf_op args[11]
  42.2 2.2 %prepare.1 = (bf16[136,80]{1,0:T(8,128)(2,1)}, bf16[2,128,16]{2,1,0:T(8,128)(2,1)}, bf16[136,80]{1,0:T(8,128)(2,1)}, bf16[2,128,16]{2,1,0:T(8,128)(2,1)}, f32[12...) custom-call(bf16[2,2,45,768]{3,2,1,0:T(8,128)(2,1)} %constant.2.clone.pick_ref, ...), custom_call_target="tpu_custom_call" | custom-call | tf_op jit(solution)/shard_map/prepare/pallas_call | solution.py:382
  44.4 0.0 collective-permute-done.2.swap_ref
  44.4 0.0 copy-start
  44.4 0.7 %copy-done = bf16[3,2,16384]{2,1,0:T(2,128)(2,1)} copy-done((bf16[3,2,16384]{2,1,0:T(2,128)(2,1)}, bf16[3,2,16384]{2,1,0:T(2,128)(2,1)S(1)}, u32[]{:S(2)}) %copy-start) | copy-done | bytes 196632
  45.0 8.2 %correct_inner.1.row_ref = f32[4,16384]{1,0:T(4,128)} custom-call(bf16[16,16384]{1,0:T(8,128)(2,1)} %get-tuple-element.27.inner_ref, bf16[3,2,16384]{2,1,0:T(2,128)(2,1)} %copy-done, f32[4,16384]{1,0:T(4,128)} %get-tuple-element.26.own_rows_ref, bf16[136,80]{1,0:T(8,128)(2,1)} %get-tuple-element.28.refs_0_, bf16[2,128,16]{2,1,0:T(8,128)(2,1)} %get-tuple-element.29.refs_1_, ...), custom_call_target="tpu_custom_call" | custom-call | tf_op jit(solution)/shard_map/correct_inner/pallas_call | solution.py:395
  53.2 0.0 collective-permute-done.4.cross_ref
  53.3 0.0 copy-start.4
  53.3 0.0 collective-permute-done.3.edge_ref
  53.3 0.0 copy-start.3
  53.3 0.6 copy-done.4
  53.9 0.0 copy-done.3
  53.9 8.8 %correct_outer.1 = f32[4,2,16384]{2,1,0:T(2,128)} custom-call(bf16[16,16384]{1,0:T(8,128)(2,1)} %get-tuple-element.22.outer_ref, bf16[3,2,16384]{2,1,0:T(2,128)(2,1)} %copy-done, bf16[4,16384]{1,0:T(4,128)(2,1)} %copy-done.3, bf16[2,16384]{1,0:T(2,128)(2,1)} %copy-done.4, f32[4,16384]{1,0:T(4,128)} %get-tuple-element.26.own_rows_ref, ...), custom_call_target="tpu_custom_call" | custom-call | tf_op jit(solution)/shard_map/correct_outer/pallas_call | solution.py:401
Async XLA Ops:
  5.3 9.4 %collective-permute-start = (f32[8,16384]{1,0:T(8,128)}, f32[8,16384]{1,0:T(8,128)S(1)}, u32[]{:S(2)}, u32[]{:S(2)}) collective-permute-start(f32[8,16384]{1,0:T(8,128)} %get-tuple-element.20.own_ref), channel_id=1, source_target_pairs={{0,2},{1,3},{4,6},{5,7},{8,10},{9,11},{12,14},{13,15},{16,18},{17,... | collective-permute-start | bytes 1572872 | tf_op jit(solution)/shard_map/ppermute | solution.py:354
  6.0 8.8 %collective-permute-start.1 = (bf16[8,16384]{1,0:T(8,128)(2,1)}, bf16[8,16384]{1,0:T(8,128)(2,1)S(1)}, u32[]{:S(2)}, u32[]{:S(2)}) collective-permute-start(bf16[8,16384]{1,0:T(8,128)(2,1)} %get-tuple-element.21), channel_id=1, source_target_pairs={{2,4},{3,5},{6,8},{7,9},{10,12},{11,13},{14,16},{15,17},{18,20},{1... | collective-permute-start | bytes 786440 | tf_op jit(solution)/shard_map/ppermute | solution.py:353
  14.7 0.7 %copy-start.2 = (bf16[8,16384]{1,0:T(8,128)(2,1)}, bf16[8,16384]{1,0:T(8,128)(2,1)S(1)}, u32[]{:S(2)}) copy-start(bf16[8,16384]{1,0:T(8,128)(2,1)S(1)} %collective-permute-done.1.far_ref) | copy-start | bytes 786436
  15.4 0.8 %copy-start.1 = (f32[8,16384]{1,0:T(8,128)}, f32[8,16384]{1,0:T(8,128)S(1)}, u32[]{:S(2)}) copy-start(f32[8,16384]{1,0:T(8,128)S(1)} %collective-permute-done.chip_ref) | copy-start | bytes 1572868
  20.9 23.5 %collective-permute-start.2 = (bf16[3,2,16384]{2,1,0:T(2,128)(2,1)}, bf16[3,2,16384]{2,1,0:T(2,128)(2,1)S(1)}, u32[]{:S(2)}, u32[]{:S(2)}) collective-permute-start(bf16[3,2,16384]{2,1,0:T(2,128)(2,1)} %get-tuple-element.23), channel_id=1, source_target_pairs={{0,1},{1,0},{2,3},{3,2},{4,5},{5,4},{6,7},{7,6},{8,9},{9,8},{10,11... | collective-permute-start | bytes 589832 | tf_op jit(solution)/shard_map/ppermute | solution.py:367
  27.6 13.9 %copy-start.5 = (bf16[128,4]{0,1:T(4,128)(2,1)S(1)}, bf16[128,4]{0,1:T(4,128)(2,1)}, u32[]{:S(2)}) copy-start(bf16[128,4]{0,1:T(4,128)(2,1)} %param.24) | copy-start | bytes 3076
  27.6 25.7 %collective-permute-start.3 = (bf16[4,16384]{1,0:T(4,128)(2,1)}, bf16[4,16384]{1,0:T(4,128)(2,1)S(1)}, u32[]{:S(2)}, u32[]{:S(2)}) collective-permute-start(bf16[4,16384]{1,0:T(4,128)(2,1)} %get-tuple-element.24), channel_id=1, source_target_pairs={{3,1},{5,3},{7,5},{9,7},{11,9},{13,11},{15,13},{17,15},{19,17},{21... | collective-permute-start | bytes 393224 | tf_op jit(solution)/shard_map/ppermute | solution.py:368
  29.8 23.4 %collective-permute-start.4 = (bf16[2,16384]{1,0:T(2,128)(2,1)}, bf16[2,16384]{1,0:T(2,128)(2,1)S(1)}, u32[]{:S(2)}, u32[]{:S(2)}) collective-permute-start(bf16[2,16384]{1,0:T(2,128)(2,1)} %get-tuple-element.25), channel_id=1, source_target_pairs={{2,1},{4,3},{6,5},{8,7},{10,9},{12,11},{14,13},{16,15},{18,17},{20... | collective-permute-start | bytes 196616 | tf_op jit(solution)/shard_map/ppermute | solution.py:374
  44.4 0.7 %copy-start = (bf16[3,2,16384]{2,1,0:T(2,128)(2,1)}, bf16[3,2,16384]{2,1,0:T(2,128)(2,1)S(1)}, u32[]{:S(2)}) copy-start(bf16[3,2,16384]{2,1,0:T(2,128)(2,1)S(1)} %collective-permute-done.2.swap_ref) | copy-start | bytes 589828
  53.3 0.6 copy-start.4
  53.3 0.7 %copy-start.3 = (bf16[4,16384]{1,0:T(4,128)(2,1)}, bf16[4,16384]{1,0:T(4,128)(2,1)S(1)}, u32[]{:S(2)}) copy-start(bf16[4,16384]{1,0:T(4,128)(2,1)S(1)} %collective-permute-done.3.edge_ref) | copy-start | bytes 393220

commit v3 on v2

--- a/solution.py
+++ b/solution.py
@@ -8,8 +8,9 @@
 from jax.experimental.pallas import tpu as pltpu
 from jax.sharding import PartitionSpec as P
 
-CENTRAL = (0.8, -0.2, 4.0 / 105.0, -1.0 / 280.0)
-BINOMIAL = (70.0, -56.0, 28.0, -8.0, 1.0)
+CENTRAL = (3.0, -32.0, 168.0, -672.0, 0.0, 672.0, -168.0, 32.0, -3.0)
+BINOMIAL = (1.0, -8.0, 28.0, -56.0, 70.0, -56.0, 28.0, -8.0, 1.0)
+CENTRAL_UNIT = 1.0 / 840.0
 DAMPING = 1.0 / 630.0
 TIME_STEP = 0.6
 EPSILON = 1e-06
@@ -22,62 +23,98 @@
 LAG = 2
 
 
-def steps(length, size, body):
-    def step(index, carry):
-        body(pl.multiple_of(index * size, size))
-        return carry
-
-    lax.fori_loop(0, length // size, step, 0)
-
-
-def upwind_change(center, pairs, signs, speeds):
-    central = jnp.zeros_like(center)
-    damping = BINOMIAL[0] * center
-    for k, (before, after) in enumerate(pairs, 1):
-        central = central + CENTRAL[k - 1] * (after - before)
-        damping = damping + BINOMIAL[k] * (after + before)
-    gradient = central + (2.0 * signs - 1.0) * (DAMPING * damping)
-    return (TIME_STEP * speeds) * gradient
+def params(**more):
+    return pltpu.CompilerParams(vmem_limit_bytes=24 << 20, **more)
 
 
 def stacked(first, second):
     return jnp.concatenate([first, second], axis=0)
 
 
-def by_row(value, row):
-    roll = functools.partial(pltpu.roll, axis=0)
-    placed = value
-    for r in range(1, 4):
-        placed = jnp.where(row == 2 * r, roll(value, r), placed)
-        placed = jnp.where(row == 2 * r - 1, roll(value, 4 + r), placed)
-    return placed
-
-
-def sweep_x(size, pot_ref, speed_ref, sign_ref, wide_ref, narrow_ref, padded):
-    length = pot_ref.shape[2]
-    padded[:, :HALO] = jnp.zeros((8, HALO), F32)
-    padded[:, HALO + length :] = jnp.zeros((8, HALO), F32)
-    padded[0:4, HALO : HALO + length] = pot_ref[0]
-    padded[4:8, HALO : HALO + length] = pot_ref[1]
-
-    def body(start):
-        here = pl.ds(start, size)
-        value = padded[:, pl.ds(start, size + 2 * HALO)]
-        sign = stacked(sign_ref[0, :, here], sign_ref[1, :, here]).astype(F32)
-        speed = stacked(speed_ref[:, here], speed_ref[:, here])
-
-        def at(k):
-            return value[:, HALO + k : HALO + k + size]
-
-        swept = at(0) - upwind_change(at(0), [(at(-k), at(k)) for k in range(1, 5)], sign, speed)
+def split(value):
+    high = value.astype(BF16).astype(F32)
+    return high, value - high
+
+
+def change_of(central, damping, signs, speeds):
+    gradient = CENTRAL_UNIT * central + ((2.0 * DAMPING) * signs - DAMPING) * damping
+    return (TIME_STEP * speeds) * gradient
+
+
+def band_matrix():
+    bands = np.zeros((3, 128, 3, 2, 128), np.float32)
+    for column in range(128):
+        for k in range(-4, 5):
+            block, lane = divmod(column + k, 128)
+            bands[0, lane, block, 0, column] = CENTRAL[k + 4]
+            bands[0, lane, block, 1, column] = BINOMIAL[k + 4]
+    return bands[0].reshape(128, 768)
+
+
+def sweep_x(blocks, band_ref, pot_ref, speed_ref, sign_ref, wide_ref, narrow_ref):
+    count = pot_ref.shape[2] // 128
+    band = stacked(band_ref[...], band_ref[...])
+
+    def tall(value):
+        return jnp.concatenate(
+            [value[:, i : i + 128] for i in range(0, value.shape[1], 128)], axis=0
+        )
+
+    for first in range(0, count, blocks):
+        start, stop = max(first - 1, 0), min(first + blocks + 1, count)
+        around = slice(128 * start, 128 * stop)
+        here = slice(128 * first, 128 * (first + blocks))
+        value = tall(stacked(pot_ref[0, :, around], pot_ref[1, :, around]))
+        zeros = jnp.zeros((8, 128), F32)
+        if start == first:
+            value = jnp.concatenate([zeros, value], axis=0)
+        if stop == first + blocks:
+            value = jnp.concatenate([value, zeros], axis=0)
+        high, rest = split(value)
+        both = jnp.concatenate([high.astype(BF16), rest.astype(BF16)], axis=1)
+        parts = jnp.dot(both, band, preferred_element_type=F32)
+        size = 8 * blocks
+        mid, before, after = slice(8, 8 + size), slice(0, size), slice(16, 16 + size)
+        total = parts[mid, :256] + parts[after, 256:512] + parts[before, 512:]
+        sign = tall(stacked(sign_ref[0, :, here], sign_ref[1, :, here]).astype(F32))
+        speed = tall(stacked(speed_ref[:, here], speed_ref[:, here]))
+        swept = value[mid] - change_of(total[:, :128], total[:, 128:], sign, speed)
+        swept = jnp.concatenate([swept[8 * i : 8 * i + 8] for i in range(blocks)], axis=1)
         wide_ref[:, here] = swept
         narrow_ref[:, here] = swept.astype(BF16)
 
-    steps(length, size, body)
+
+def column_matrix():
+    rows = np.zeros((2, 2, 7, 8, 64), np.float32)
+    for odd in range(2):
+        for section in range(2):
+            part = rows[odd, section]
+            for place in range(4):
+                r = 3 - place if section else place
+                for g in range(2):
+                    at, own = 2 * place + g, 4 * g + r
+                    for k in range(-4, 5):
+                        block, source = divmod(r + k, 4)
+                        if block == 0:
+                            starts = (0, 8)
+                        elif (block < 0) == bool(odd):
+                            starts = (16, 24)
+                        else:
+                            starts = (32,)
+                        for start in starts:
+                            part[0, at, start + 4 * g + source] = CENTRAL[k + 4]
+                            part[1, at, start + 4 * g + source] = BINOMIAL[k + 4]
+                    part[2, at, [own, 8 + own]] = 1.0
+                    part[3, at, 40 + own] = 1.0
+                    part[4, at, [48 + r, 56 + r]] = 1.0
+                    part[5, at, [52 + r, 60 + r]] = 1.0
+                part[6, 4 + place, [52 + r, 60 + r]] = 1.0
+    return rows.reshape(2, 2, 56, 64)
 
 
 def sweep_y(
     size,
+    column_ref,
     own_ref,
     chip_ref,
     far_ref,
@@ -91,52 +128,35 @@
     edge_ref,
     cross_ref,
 ):
-    odd = lax.rem(lax.axis_index("wide"), 2) == 1
-    low = lax.axis_index("section") == 0
-
-    def body(start):
-        here = pl.ds(start, size)
-        own, chip, far = own_ref[:, here], chip_ref[:, here], far_ref[:, here].astype(F32)
-        below = jnp.where(odd, chip, far)
-        above = jnp.where(odd, far, chip)
+    columns = column_ref[lax.rem(lax.axis_index("wide"), 2), lax.axis_index("section")]
+    row = lax.broadcasted_iota(jnp.int32, (8, size), 0)
+    for start in range(0, own_ref.shape[1], size):
+        here = slice(start, start + size)
         sign = stacked(sign_ref[0, :, here], sign_ref[1, :, here]).astype(F32)
-        speed = stacked(speed_ref[:, here], speed_ref[:, here])
-        crowd = density_ref[:, here]
-        density = stacked(crowd, crowd)
-        row = lax.broadcasted_iota(jnp.int32, (8, size), 0)
-        in_group = row % 4
-        roll = functools.partial(pltpu.roll, axis=0)
-        pairs = []
-        for k in range(1, 5):
-            if k == 4:
-                pairs.append((below, above))
-            else:
-                before = jnp.where(in_group < 4 - k, own, below)
-                before = jnp.where(in_group >= k, roll(before, k), roll(before, 4 + k))
-                after = jnp.where(in_group >= k, own, above)
-                after = jnp.where(in_group < 4 - k, roll(after, 8 - k), roll(after, 4 - k))
-                pairs.append((before, after))
-        physics = own - upwind_change(own, pairs, sign, speed) + TIME_STEP * density
-        physics = by_row(physics, row)
-        crowd = jnp.where(row >= 4, density, 0.0)
-        up_2, up_4, up_6 = roll(physics, 2), roll(physics, 4), roll(physics, 6)
-        own_rows_ref[:, here] = jnp.where(low, physics, up_4)[0:4]
-        window = jnp.where(row < 6, jnp.where(low, physics, up_6), 0.0)
-        window_crowd = jnp.where(low, crowd, roll(crowd, 7))
-        inner_ref[:, here] = jnp.concatenate([window, window_crowd], axis=0).astype(BF16)
-        flipped = jnp.where(low, up_2, jnp.where(row < 4, up_4, physics))
-        flipped_crowd = jnp.where(low, crowd, jnp.where(row == 4, roll(crowd, 5), roll(crowd, 7)))
-        outer_ref[:, here] = jnp.concatenate([flipped, flipped_crowd], axis=0).astype(BF16)
-        given = jnp.where(low, up_6, physics).astype(BF16)
+        sources = (
+            split(own_ref[:, here])
+            + split(chip_ref[:, here])
+            + (far_ref[:, here].astype(F32), sign)
+            + split(stacked(speed_ref[:, here], density_ref[:, here]))
+        )
+        sources = jnp.concatenate(
+            [stacked(sources[i], sources[i + 1]).astype(BF16) for i in range(0, 8, 2)], axis=0
+        )
+        parts = jnp.dot(columns, sources, preferred_element_type=F32)
+        central, damping, own, sign, speed, density, crowd = (
+            parts[8 * i : 8 * i + 8] for i in range(7)
+        )
+        physics = own - change_of(central, damping, sign, speed) + TIME_STEP * density
+        turned = pltpu.roll(physics, 2, axis=0)
+        own_rows_ref[:, here] = physics[0:4]
+        inner_ref[:, here] = stacked(physics, crowd).astype(BF16)
+        outer_ref[:, here] = stacked(turned, crowd).astype(BF16)
+        narrow = physics.astype(BF16)
         for j in range(3):
-            swap_ref[j, :, here] = given[2 * j : 2 * j + 2]
-        edge = jnp.where(low, up_2, physics)
-        edge_crowd = jnp.where(low, roll(crowd, 3), roll(crowd, 6))
-        edge = jnp.where(row < 2, edge, jnp.where(row == 2, edge_crowd, 0.0))
+            swap_ref[j, :, here] = narrow[2 * j + 2 : 2 * j + 4]
+        edge = jnp.where(row < 2, turned, pltpu.roll(crowd, 3, axis=0))
         edge_ref[:, here] = edge[0:4].astype(BF16)
-        cross_ref[:, here] = jnp.where(low, physics, up_2)[0:2].astype(BF16)
-
-    steps(own_ref.shape[1], size, body)
+        cross_ref[:, here] = narrow[0:2]
 
 
 def mix_features(size, start, length, features, mix_ref, fix_ref):
@@ -216,10 +236,10 @@
     clear_rims(features, length)
     features[:, mid] = inner_ref[...]
     for j in range(3):
-        features[6 + 2 * j : 8 + 2 * j, mid] = swap_ref[j]
+        features[6 + 2 * j : 8 + 2 * j, mid] = swap_ref[2 - j]
 
     def finish(here, change):
-        own = jnp.where(low, own_rows_ref[2:4, here], own_rows_ref[0:2, here])
+        own = own_rows_ref[2:4, here]
         out_ref[:, here] = change + in_groups(low, own, swap_ref[1, :, here])
 
     correct(size, length, features, weight_refs, finish)
@@ -239,20 +259,10 @@
     features[6:8, mid] = cross_ref[...]
     features[10:12, mid] = swap_ref[1]
 
-    @pl.when(low)
-    def _():
-        features[8:10, mid] = swap_ref[0]
-
-    @pl.when(jnp.logical_not(low))
-    def _():
-        features[8:10, mid] = swap_ref[2]
+    features[8:10, mid] = swap_ref[2]
 
     def finish(here, change):
-        own = jnp.where(low, own_rows_ref[0:2, here], own_rows_ref[2:4, here])
-        other = jnp.where(
-            low, swap_ref[0, :, here].astype(F32), swap_ref[2, :, here].astype(F32)
-        )
-        outer_row = change + in_groups(low, own, other)
+        outer_row = change + in_groups(low, own_rows_ref[0:2, here], swap_ref[2, :, here])
         inner_row = row_ref[:, here]
         out_ref[:, 0, here] = jnp.where(low, outer_row, inner_row)
         out_ref[:, 1, here] = jnp.where(low, inner_row, outer_row)
@@ -268,7 +278,7 @@
             for row in range(3):
                 for group in range(4):
                     other = int(group // 2 != section)
-                    shift = 2 - row if outer and section else row
+                    shift = 2 - row if section else row
                     places.append((6 * other + 2 * row + group % 2, shift, group))
                 crowd = 12 + ((row + 2) % 3 if outer else row)
                 places.append((crowd, shift, 4))
@@ -295,10 +305,6 @@
     def unit(size):
         rows = lax.broadcasted_iota(jnp.int32, (size, size), 0)
         return jnp.where(rows == lax.broadcasted_iota(jnp.int32, (size, size), 1), 1.0, 0.0)
-
-    def split(value):
-        high = value.astype(BF16)
-        return high, (value - high.astype(F32)).astype(BF16)
 
     conv = turned(conv_ref[0], unit(3).astype(BF16))
     for outer, (mix_out, fix_out) in enumerate((inner_refs, outer_refs)):
@@ -333,7 +339,7 @@
     out_weight,
 ):
     length = potential.shape[2]
-    size = min(length, 4096)
+    size = min(length, 2048)
     chunk = min(length, 512)
     blocks = lax.axis_size("wide")
     shape = jax.ShapeDtypeStruct
@@ -343,15 +349,30 @@
         return pairs + [(b, a) for a, b in pairs]
 
     swept, narrow = pl.pallas_call(
-        functools.partial(sweep_x, size),
+        functools.partial(sweep_x, size // 128),
         out_shape=(shape((8, length), F32), shape((8, length), BF16)),
-        scratch_shapes=[
-            pltpu.VMEM((8, length + 2 * HALO), F32),
-        ],
+        compiler_params=params(),
         name="sweep_x",
-    )(potential, speed_x, sign_x)
+    )(jnp.asarray(band_matrix(), BF16), potential, speed_x, sign_x)
     far = lax.ppermute(narrow, BOTH, swaps(1))
     chip = lax.ppermute(swept, BOTH, swaps(0))
+    mix_shapes = (shape((136, 80), BF16), shape((2, 128, 16), BF16))
+    shared_shapes = (shape((128, 1), F32), shape((256, 128), BF16), shape((8, 256), BF16))
+    made = pl.pallas_call(
+        prepare,
+        out_shape=mix_shapes + mix_shapes + shared_shapes,
+        compiler_params=params(),
+        name="prepare",
+    )(
+        jnp.asarray(selections(), BF16),
+        stem_weight,
+        conv_weight,
+        norm_gain,
+        up_weight,
+        down_weight,
+        out_weight,
+    )
+    chip, far, made = lax.optimization_barrier((chip, far, made))
     own_rows, inner, outer, given, edge, cross = pl.pallas_call(
         functools.partial(sweep_y, size),
         out_shape=(
@@ -362,8 +383,9 @@
             shape((4, length), BF16),
             shape((2, length), BF16),
         ),
+        compiler_params=params(),
         name="sweep_y",
-    )(swept, chip, far, speed_y, sign_y, density)
+    )(jnp.asarray(column_matrix(), BF16), swept, chip, far, speed_y, sign_y, density)
     swap = lax.ppermute(given, "section", [(0, 1), (1, 0)])
     edge = lax.ppermute(
         edge,
@@ -377,31 +399,20 @@
         [(2 * w, 2 * w - 1) for w in range(1, blocks)]
         + [(2 * w + 1, 2 * w + 2) for w in range(blocks - 1)],
     )
-    mix_shapes = (shape((136, 80), BF16), shape((2, 128, 16), BF16))
-    shared_shapes = (shape((128, 1), F32), shape((256, 128), BF16), shape((8, 256), BF16))
-    made = pl.pallas_call(
-        prepare, out_shape=mix_shapes + mix_shapes + shared_shapes, name="prepare"
-    )(
-        jnp.asarray(selections(), BF16),
-        stem_weight,
-        conv_weight,
-        norm_gain,
-        up_weight,
-        down_weight,
-        out_weight,
-    )
     inner_weights, outer_weights = made[0:2] + made[4:7], made[2:7]
     scratch = [pltpu.VMEM((16, length + 2 * HALO), BF16)]
     row = pl.pallas_call(
         functools.partial(correct_inner, chunk),
         out_shape=shape((4, length), F32),
         scratch_shapes=scratch,
+        compiler_params=params(),
         name="correct_inner",
     )(inner, swap, own_rows, *inner_weights)
     return pl.pallas_call(
         functools.partial(correct_outer, chunk),
         out_shape=shape((4, 2, length), F32),
         scratch_shapes=scratch,
+        compiler_params=params(),
         name="correct_outer",
     )(outer, swap, edge, cross, own_rows, row, *outer_weights)
 

time: 63 us -> 49.8 us (0.79)
  Pallas kernels: 29.1 us -> 15.4 us
  waiting for transfers between devices: 5.35 us -> 4.41 us
    pallas_call x1, Pallas kernels: 5.28 us -> 0.65 us  [shards(): pl.pallas_call(functools.partial(sweep_x, size // 128), out_shape=(shape(...]
    pallas_call x1, Pallas kernels: 4.58 us -> 0.75 us  [shards(): pl.pallas_call(functools.partial(sweep_y, size), out_shape=(shape((4, len...]
    pallas_call x1, Pallas kernels: 8.22 us -> 6.29 us  [shards(): pl.pallas_call(functools.partial(correct_inner, chunk), out_shape=shape((...]
    pallas_call x1, Pallas kernels: 2.17 us -> 0.48 us  [shards(): pl.pallas_call(prepare, out_shape=mix_shapes + mix_shapes + shared_shapes...]
    pallas_call x1, Pallas kernels: 8.84 us -> 7.18 us  [shards(): pl.pallas_call(functools.partial(correct_outer, chunk), out_shape=shape((...]
    ppermute x1, waiting for transfers between devices: 5.34 us -> 4.4 us  [shards(): far = lax.ppermute(narrow, BOTH, swaps(1))]
    unnamed x13 -> x31, local copies, waits for them, and re-layouts: 3.6 us -> 4.14 us
  transfers between devices with their start and end apart: 5 -> 5, of which waited for: 1 -> 1; matrix products, arithmetic and copies ran while one was open for 1% -> 0% of each run, Pallas kernels for 17% -> 14%
where the time goes in v3:
time: 49.8 us; the launch traced here: 49 us
  starting transfers between devices  24.9 us (50%)
  Pallas kernels  15.4 us (31%)
  waiting for transfers between devices  4.41 us (9%)
  local copies, waits for them, and re-layouts  4.14 us (8%)
    ppermute x1, starting transfers between devices, shards(): lax.ppermute(cross, BOTH, [(2 * w, 2 * w - 1) for w in range(1, blocks)]...  11.8 us
    pallas_call x1, Pallas kernels, shards(): pl.pallas_call(functools.partial(correct_outer, chunk), out_shape=shape((...  7.18 us
    ppermute x1, starting transfers between devices, shards(): swap = lax.ppermute(given, 'section', [(0, 1), (1, 0)])  6.77 us
    pallas_call x1, Pallas kernels, shards(): pl.pallas_call(functools.partial(correct_inner, chunk), out_shape=shape((...  6.29 us
    ppermute x1, waiting for transfers between devices, shards(): far = lax.ppermute(narrow, BOTH, swaps(1))  4.4 us
    unnamed x31, local copies, waits for them, and re-layouts  4.14 us
    ppermute x1, starting transfers between devices, shards(): far = lax.ppermute(narrow, BOTH, swaps(1))  3.44 us
    ppermute x1, starting transfers between devices, shards(): lax.ppermute(edge, BOTH, [(2 * w + 1, 2 * w - 1) for w in range(1, blocks...  2.17 us
  transfers between devices with their start and end apart: 5, of which 1 were waited for; matrix products, arithmetic and copies ran while one was open for 0% of the time, Pallas kernels for 14%

profile of v3, /device:TPU:7, one launch (start us, length us, event | category | flops | bytes accessed | tf_op | source)
XLA Modules:
  0.0 49.0 jit_solution(12090994420778737415)
XLA Ops:
  0.0 0.0 copy-start
  0.0 1.0 %copy-done = f32[2,4,16384]{2,1,0:T(4,128)S(1)} copy-done((f32[2,4,16384]{2,1,0:T(4,128)S(1)}, f32[2,4,16384]{2,1,0:T(4,128)}, u32[]{:S(2)}) %copy-start) | copy-done | bytes 524312
  1.0 0.0 copy-start.1
  1.0 1.0 %copy-done.1 = s32[2,4,16384]{2,1,0:T(4,128)S(1)} copy-done((s32[2,4,16384]{2,1,0:T(4,128)S(1)}, s32[2,4,16384]{2,1,0:T(4,128)}, u32[]{:S(2)}) %copy-start.1) | copy-done | bytes 524312
  2.1 0.0 copy-start.6
  2.1 0.9 %copy-done.6 = f32[4,16384]{1,0:T(4,128)S(1)} copy-done((f32[4,16384]{1,0:T(4,128)S(1)}, f32[4,16384]{1,0:T(4,128)}, u32[]{:S(2)}) %copy-start.6) | copy-done | bytes 262168
  3.0 0.0 copy-start.7
  3.0 0.9 %copy-done.7 = bf16[128,768]{1,0:T(8,128)(2,1)S(1)} copy-done((bf16[128,768]{1,0:T(8,128)(2,1)S(1)}, bf16[128,768]{1,0:T(8,128)(2,1)}, u32[]{:S(2)}) %copy-start.7) | copy-done | bytes 196632
  4.0 0.0 copy-start.14
  4.0 0.0 copy-start.3
  4.0 0.0 copy-start.8
  4.0 0.0 copy-start.9
  4.0 0.0 copy-start.11
  4.0 0.0 copy-start.12
  4.0 0.0 copy-start.13
  4.0 0.0 copy-start.2
  4.0 0.0 copy-start.5
  4.0 0.6 %sweep_x.1 = (f32[8,16384]{1,0:T(8,128)S(1)}, bf16[8,16384]{1,0:T(8,128)(2,1)S(1)}) custom-call(bf16[128,768]{1,0:T(8,128)(2,1)S(1)} %copy-done.7, f32[2,4,16384]{2,1,0:T(4,128)S(1)} %copy-done, f32[4,16384]{1,0:T(4,128)S(1)} %copy-done.6, s32[2,4,16384]{2,1,0:T(4,128)S(1)} %copy-done.1), custom_call_target="tpu_custom_call" | custom-call | tf_op jit(solution)/shard_map/sweep_x/pallas_call | solution.py:351
  4.7 0.0 copy-start.4
  4.7 0.8 %collective-permute-start = (f32[8,16384]{1,0:T(8,128)S(1)}, f32[8,16384]{1,0:T(8,128)S(1)}, u32[]{:S(2)}, u32[]{:S(2)}) collective-permute-start(f32[8,16384]{1,0:T(8,128)S(1)} %get-tuple-element.29.own_ref), channel_id=1, source_target_pairs={{0,2},{1,3},{4,6},{5,7},{8,10},{9,11},{12,14},{13,15},{16,18},{17,... | collective-permute-start | bytes 1572872 | tf_op jit(solution)/shard_map/ppermute | solution.py:358
  5.5 3.4 %collective-permute-start.1 = (bf16[8,16384]{1,0:T(8,128)(2,1)S(1)}, bf16[8,16384]{1,0:T(8,128)(2,1)S(1)}, u32[]{:S(2)}, u32[]{:S(2)}) collective-permute-start(bf16[8,16384]{1,0:T(8,128)(2,1)S(1)} %get-tuple-element.30), channel_id=1, source_target_pairs={{2,4},{3,5},{6,8},{7,9},{10,12},{11,13},{14,16},{15,17},{18,20},{1... | collective-permute-start | bytes 786440 | tf_op jit(solution)/shard_map/ppermute | solution.py:357
  8.9 0.0 copy-done.14
  8.9 0.1 copy.16.out_ref
  9.1 0.0 copy-done.3
  9.1 0.0 copy-done.8
  9.1 0.0 copy-done.9
  9.1 0.0 copy-done.11
  9.1 0.0 copy-done.12
  9.1 0.0 copy-done.13
  9.1 0.0 copy-start.10
  9.1 0.5 prepare.1
  9.6 4.4 %collective-permute-done.1.far_ref = bf16[8,16384]{1,0:T(8,128)(2,1)S(1)} collective-permute-done((bf16[8,16384]{1,0:T(8,128)(2,1)S(1)}, bf16[8,16384]{1,0:T(8,128)(2,1)S(1)}, u32[]{:S(2)}, u32[]{:S(2)}) %collective-permute-start.1) | collective-permute-done | bytes 262176 | tf_op jit(solution)/shard_map/ppermute | solution.py:357
  14.0 0.0 collective-permute-done.chip_ref
  14.0 0.0 copy-done.2
  14.0 0.0 copy-done.5
  14.0 0.0 copy-done.4
  14.0 0.0 copy-done.10
  14.0 0.8 %sweep_y.1 = (f32[4,16384]{1,0:T(4,128)S(1)}, bf16[16,16384]{1,0:T(8,128)(2,1)S(1)}, bf16[16,16384]{1,0:T(8,128)(2,1)S(1)}, bf16[3,2,16384]{2,1,0:T(2,128)(2,1)S...) custom-call(bf16[2,2,56,64]{3,2,1,0:T(8,128)(2,1)S(1)} %copy-done.10, ...), custom_call_target="tpu_custom_call" | custom-call | tf_op jit(solution)/shard_map/sweep_y/pallas_call | solution.py:376
  14.8 6.8 %collective-permute-start.2 = (bf16[3,2,16384]{2,1,0:T(2,128)(2,1)S(1)}, bf16[3,2,16384]{2,1,0:T(2,128)(2,1)S(1)}, u32[]{:S(2)}, u32[]{:S(2)}) collective-permute-start(bf16[3,2,16384]{2,1,0:T(2,128)(2,1)S(1)} %get-tuple-element.41), channel_id=1, source_target_pairs={{0,1},{1,0},{2,3},{3,2},{4,5},{5,4},{6,7},{7,6},{8,9},{9,8},{10,11... | collective-permute-start | bytes 589832 | tf_op jit(solution)/shard_map/ppermute | solution.py:389
  21.6 2.2 %collective-permute-start.3 = (bf16[4,16384]{1,0:T(4,128)(2,1)S(1)}, bf16[4,16384]{1,0:T(4,128)(2,1)S(1)}, u32[]{:S(2)}, u32[]{:S(2)}) collective-permute-start(bf16[4,16384]{1,0:T(4,128)(2,1)S(1)} %get-tuple-element.42), channel_id=1, source_target_pairs={{3,1},{5,3},{7,5},{9,7},{11,9},{13,11},{15,13},{17,15},{19,17},{21... | collective-permute-start | bytes 393224 | tf_op jit(solution)/shard_map/ppermute | solution.py:390
  23.7 11.8 %collective-permute-start.4 = (bf16[2,16384]{1,0:T(2,128)(2,1)S(1)}, bf16[2,16384]{1,0:T(2,128)(2,1)S(1)}, u32[]{:S(2)}, u32[]{:S(2)}) collective-permute-start(bf16[2,16384]{1,0:T(2,128)(2,1)S(1)} %get-tuple-element.43), channel_id=1, source_target_pairs={{2,1},{4,3},{6,5},{8,7},{10,9},{12,11},{14,13},{16,15},{18,17},{20... | collective-permute-start | bytes 196616 | tf_op jit(solution)/shard_map/ppermute | solution.py:396
  35.5 0.0 collective-permute-done.2.swap_ref
  35.5 6.3 %correct_inner.1.row_ref = f32[4,16384]{1,0:T(4,128)S(1)} custom-call(bf16[16,16384]{1,0:T(8,128)(2,1)S(1)} %get-tuple-element.45.inner_ref, bf16[3,2,16384]{2,1,0:T(2,128)(2,1)S(1)} %collective-permute-done.2.swap_ref, f32[4,16384]{1,0:T(4,128)S(1)} %get-tuple-element.44.own_rows_ref, bf16[136,80]{1,0:T(8,128)(2,1)S(1)} %get-tuple-element.46.refs_0_, ...), custom_call_target="tpu_custom_call" | custom-call | tf_op jit(solution)/shard_map/correct_inner/pallas_call | solution.py:404
  41.8 0.0 collective-permute-done.4.cross_ref
  41.8 0.0 collective-permute-done.3.edge_ref
  41.8 7.2 %correct_outer.1 = f32[4,2,16384]{2,1,0:T(2,128)} custom-call(bf16[16,16384]{1,0:T(8,128)(2,1)S(1)} %get-tuple-element.40.outer_ref, bf16[3,2,16384]{2,1,0:T(2,128)(2,1)S(1)} %collective-permute-done.2.swap_ref, bf16[4,16384]{1,0:T(4,128)(2,1)S(1)} %collective-permute-done.3.edge_ref, bf16[2,16384]{1,0:T(2,128)(2,1)S(1)} %collective-permute-done.4.cross_ref, ...), custom_call_target="tpu_custom_call" | custom-call | tf_op jit(solution)/shard_map/correct_outer/pallas_call | solution.py:411
Async XLA Ops:
  0.0 1.0 %copy-start = (f32[2,4,16384]{2,1,0:T(4,128)S(1)}, f32[2,4,16384]{2,1,0:T(4,128)}, u32[]{:S(2)}) copy-start(f32[2,4,16384]{2,1,0:T(4,128)} %pot_ref.1) | copy-start | bytes 1572868
  1.0 1.0 %copy-start.1 = (s32[2,4,16384]{2,1,0:T(4,128)S(1)}, s32[2,4,16384]{2,1,0:T(4,128)}, u32[]{:S(2)}) copy-start(s32[2,4,16384]{2,1,0:T(4,128)} %sign_ref.2) | copy-start | bytes 1572868
  2.1 0.9 %copy-start.6 = (f32[4,16384]{1,0:T(4,128)S(1)}, f32[4,16384]{1,0:T(4,128)}, u32[]{:S(2)}) copy-start(f32[4,16384]{1,0:T(4,128)} %speed_ref.2) | copy-start | bytes 786436
  3.0 0.9 %copy-start.7 = (bf16[128,768]{1,0:T(8,128)(2,1)S(1)}, bf16[128,768]{1,0:T(8,128)(2,1)}, u32[]{:S(2)}) copy-start(bf16[128,768]{1,0:T(8,128)(2,1)} %constant.6.clone.band_ref) | copy-start | bytes 589828
  4.0 4.9 %copy-start.14 = (bf16[128,4]{0,1:T(4,128)(2,1)S(1)}, bf16[128,4]{0,1:T(4,128)(2,1)}, u32[]{:S(2)}) copy-start(bf16[128,4]{0,1:T(4,128)(2,1)} %param.26) | copy-start | bytes 3076
  4.0 5.1 %copy-start.3 = (bf16[2,2,45,768]{3,2,1,0:T(8,128)(2,1)S(1)}, bf16[2,2,45,768]{3,2,1,0:T(8,128)(2,1)}, u32[]{:S(2)}) copy-start(bf16[2,2,45,768]{3,2,1,0:T(8,128)(2,1)} %constant.7.clone.pick_ref) | copy-start | bytes 829444
  4.0 5.1 %copy-start.8 = (bf16[1,128,256]{2,1,0:T(8,128)(2,1)S(1)}, bf16[1,128,256]{2,1,0:T(8,128)(2,1)}, u32[]{:S(2)}) copy-start(bf16[1,128,256]{2,1,0:T(8,128)(2,1)} %up_ref.1) | copy-start | bytes 196612
  4.0 5.1 %copy-start.9 = (bf16[1,256,128]{2,1,0:T(8,128)(2,1)S(1)}, bf16[1,256,128]{2,1,0:T(8,128)(2,1)}, u32[]{:S(2)}) copy-start(bf16[1,256,128]{2,1,0:T(8,128)(2,1)} %down_ref.1) | copy-start | bytes 196612
  4.0 5.1 %copy-start.11 = (bf16[45,128]{1,0:T(8,128)(2,1)S(1)}, bf16[45,128]{1,0:T(8,128)(2,1)}, u32[]{:S(2)}) copy-start(bf16[45,128]{1,0:T(8,128)(2,1)} %stem_ref.1) | copy-start | bytes 34564
  4.0 5.1 %copy-start.12 = (bf16[1,3,128]{2,1,0:T(4,128)(2,1)S(1)}, bf16[1,3,128]{2,1,0:T(4,128)(2,1)}, u32[]{:S(2)}) copy-start(bf16[1,3,128]{2,1,0:T(4,128)(2,1)} %conv_ref.1) | copy-start | bytes 2308
  4.0 5.1 %copy-start.13 = (f32[1,128]{1,0:T(1,128)S(1)}, f32[1,128]{1,0:T(1,128)}, u32[]{:S(2)}) copy-start(f32[1,128]{1,0:T(1,128)} %gain_ref.1) | copy-start | bytes 1540
  4.0 10.0 %copy-start.2 = (s32[2,4,16384]{2,1,0:T(4,128)S(1)}, s32[2,4,16384]{2,1,0:T(4,128)}, u32[]{:S(2)}) copy-start(s32[2,4,16384]{2,1,0:T(4,128)} %sign_ref.3) | copy-start | bytes 1572868
  4.0 10.0 %copy-start.5 = (f32[4,16384]{1,0:T(4,128)S(1)}, f32[4,16384]{1,0:T(4,128)}, u32[]{:S(2)}) copy-start(f32[4,16384]{1,0:T(4,128)} %density_ref.1) | copy-start | bytes 786436
  4.7 9.3 %copy-start.4 = (f32[4,16384]{1,0:T(4,128)S(1)}, f32[4,16384]{1,0:T(4,128)}, u32[]{:S(2)}) copy-start(f32[4,16384]{1,0:T(4,128)} %speed_ref.3) | copy-start | bytes 786436
  4.7 9.3 %collective-permute-start = (f32[8,16384]{1,0:T(8,128)S(1)}, f32[8,16384]{1,0:T(8,128)S(1)}, u32[]{:S(2)}, u32[]{:S(2)}) collective-permute-start(f32[8,16384]{1,0:T(8,128)S(1)} %get-tuple-element.29.own_ref), channel_id=1, source_target_pairs={{0,2},{1,3},{4,6},{5,7},{8,10},{9,11},{12,14},{13,15},{16,18},{17,... | collective-permute-start | bytes 1572872 | tf_op jit(solution)/shard_map/ppermute | solution.py:358
  5.5 8.6 %collective-permute-start.1 = (bf16[8,16384]{1,0:T(8,128)(2,1)S(1)}, bf16[8,16384]{1,0:T(8,128)(2,1)S(1)}, u32[]{:S(2)}, u32[]{:S(2)}) collective-permute-start(bf16[8,16384]{1,0:T(8,128)(2,1)S(1)} %get-tuple-element.30), channel_id=1, source_target_pairs={{2,4},{3,5},{6,8},{7,9},{10,12},{11,13},{14,16},{15,17},{18,20},{1... | collective-permute-start | bytes 786440 | tf_op jit(solution)/shard_map/ppermute | solution.py:357
  9.1 4.9 %copy-start.10 = (bf16[2,2,56,64]{3,2,1,0:T(8,128)(2,1)S(1)}, bf16[2,2,56,64]{3,2,1,0:T(8,128)(2,1)}, u32[]{:S(2)}) copy-start(bf16[2,2,56,64]{3,2,1,0:T(8,128)(2,1)} %constant.8.clone.column_ref) | copy-start | bytes 86020
  14.8 20.7 %collective-permute-start.2 = (bf16[3,2,16384]{2,1,0:T(2,128)(2,1)S(1)}, bf16[3,2,16384]{2,1,0:T(2,128)(2,1)S(1)}, u32[]{:S(2)}, u32[]{:S(2)}) collective-permute-start(bf16[3,2,16384]{2,1,0:T(2,128)(2,1)S(1)} %get-tuple-element.41), channel_id=1, source_target_pairs={{0,1},{1,0},{2,3},{3,2},{4,5},{5,4},{6,7},{7,6},{8,9},{9,8},{10,11... | collective-permute-start | bytes 589832 | tf_op jit(solution)/shard_map/ppermute | solution.py:389
  21.6 20.3 %collective-permute-start.3 = (bf16[4,16384]{1,0:T(4,128)(2,1)S(1)}, bf16[4,16384]{1,0:T(4,128)(2,1)S(1)}, u32[]{:S(2)}, u32[]{:S(2)}) collective-permute-start(bf16[4,16384]{1,0:T(4,128)(2,1)S(1)} %get-tuple-element.42), channel_id=1, source_target_pairs={{3,1},{5,3},{7,5},{9,7},{11,9},{13,11},{15,13},{17,15},{19,17},{21... | collective-permute-start | bytes 393224 | tf_op jit(solution)/shard_map/ppermute | solution.py:390
  23.7 18.1 %collective-permute-start.4 = (bf16[2,16384]{1,0:T(2,128)(2,1)S(1)}, bf16[2,16384]{1,0:T(2,128)(2,1)S(1)}, u32[]{:S(2)}, u32[]{:S(2)}) collective-permute-start(bf16[2,16384]{1,0:T(2,128)(2,1)S(1)} %get-tuple-element.43), channel_id=1, source_target_pairs={{2,1},{4,3},{6,5},{8,7},{10,9},{12,11},{14,13},{16,15},{18,17},{20... | collective-permute-start | bytes 196616 | tf_op jit(solution)/shard_map/ppermute | solution.py:396

commit v4 on v3

--- a/solution.py
+++ b/solution.py
@@ -14,8 +14,8 @@
 DAMPING = 1.0 / 630.0
 TIME_STEP = 0.6
 EPSILON = 1e-06
-GELU_0 = 0.7978845608028654
-GELU_1 = GELU_0 * 0.044715
+GELU_LINEAR = 0.7978845608028654
+GELU_SCALE = (GELU_LINEAR * 0.044715) ** (1.0 / 3.0)
 BF16 = jnp.bfloat16
 F32 = jnp.float32
 BOTH = ("wide", "section")
@@ -23,8 +23,8 @@
 LAG = 2
 
 
-def params(**more):
-    return pltpu.CompilerParams(vmem_limit_bytes=24 << 20, **more)
+def params(mebibytes=24):
+    return pltpu.CompilerParams(vmem_limit_bytes=mebibytes << 20)
 
 
 def stacked(first, second):
@@ -51,8 +51,39 @@
     return bands[0].reshape(128, 768)
 
 
-def sweep_x(blocks, band_ref, pot_ref, speed_ref, sign_ref, wide_ref, narrow_ref):
+def sweep_x(
+    blocks,
+    band_hbm,
+    pot_hbm,
+    speed_hbm,
+    sign_hbm,
+    wide_ref,
+    narrow_ref,
+    band_ref,
+    pot_ref,
+    speed_ref,
+    sign_ref,
+    band_sem,
+    sems,
+):
     count = pot_ref.shape[2] // 128
+    pieces = count // blocks
+    copies = [[] for _ in range(pieces)]
+    band_copy = pltpu.make_async_copy(band_hbm, band_ref, band_sem)
+    for i in range(pieces):
+        here = slice(128 * blocks * i, 128 * blocks * (i + 1))
+        for j, (source, target) in enumerate(
+            ((pot_hbm, pot_ref), (sign_hbm, sign_ref), (speed_hbm, speed_ref))
+        ):
+            cut = (slice(None),) * (len(source.shape) - 1) + (here,)
+            copies[i].append(
+                pltpu.make_async_copy(source.at[cut], target.at[cut], sems.at[i, j])
+            )
+            copies[i][j].start()
+        if i == 0:
+            band_copy.start()
+    band_copy.wait()
+    copies[0][0].wait()
     band = stacked(band_ref[...], band_ref[...])
 
     def tall(value):
@@ -61,6 +92,9 @@
         )
 
     for first in range(0, count, blocks):
+        i = first // blocks
+        for copy in copies[i][1:] + [c[0] for c in copies[i + 1 : i + 2]]:
+            copy.wait()
         start, stop = max(first - 1, 0), min(first + blocks + 1, count)
         around = slice(128 * start, 128 * stop)
         here = slice(128 * first, 128 * (first + blocks))
@@ -182,21 +216,19 @@
     return mixed, change
 
 
-def normalise(mixed, gain):
+def normalise(mixed):
     square = jnp.sum(mixed * mixed, axis=0, keepdims=True)
     inverse = lax.rsqrt(square * (1.0 / 128.0) + EPSILON)
-    return (mixed * inverse * gain).astype(BF16)
-
-
-def lift_twice(normed, up_ref):
+    return (mixed * inverse).astype(BF16)
+
+
+def lift_scaled(normed, up_ref):
     lift = jnp.dot(up_ref[...], normed, preferred_element_type=F32).astype(BF16)
-    inner = BF16(GELU_0) + BF16(GELU_1) * (lift * lift)
-    return lift + lift * jnp.tanh(lift * inner)
+    return lift + lift * jnp.tanh(lift * (lift * lift + BF16(GELU_LINEAR / GELU_SCALE)))
 
 
 def correct(size, length, features, weight_refs, finish):
-    mix_ref, fix_ref, gain_ref, up_ref, down_ref = weight_refs
-    gain = jnp.broadcast_to(gain_ref[...], (128, size))
+    mix_ref, fix_ref, up_ref, down_ref = weight_refs
     count = length // size
     mixed, normed, lifted, changes = {}, {}, {}, {}
     for t in range(count + 3 * LAG):
@@ -210,10 +242,10 @@
             finish(slice(u * size, u * size + size), changes.pop(u) + (result[0:4] + result[4:8]))
         u = t - 2 * LAG
         if 0 <= u < count:
-            lifted[u] = lift_twice(normed.pop(u), up_ref)
+            lifted[u] = lift_scaled(normed.pop(u), up_ref)
         u = t - LAG
         if 0 <= u < count:
-            normed[u] = normalise(mixed.pop(u), gain)
+            normed[u] = normalise(mixed.pop(u))
 
 
 def in_groups(low, own, other):
@@ -248,8 +280,10 @@
 def correct_outer(
     size, outer_ref, swap_ref, edge_ref, cross_ref, own_rows_ref, row_ref, *refs
 ):
-    *weight_refs, out_ref, features = refs
+    *weight_refs, out_hbm, features, out_ref, sems = refs
     length = outer_ref.shape[1]
+    part = length // sems.shape[0]
+    copies = []
     low = lax.axis_index("section") == 0
     mid = slice(HALO, HALO + length)
     clear_rims(features, length)
@@ -266,8 +300,16 @@
         inner_row = row_ref[:, here]
         out_ref[:, 0, here] = jnp.where(low, outer_row, inner_row)
         out_ref[:, 1, here] = jnp.where(low, inner_row, outer_row)
+        if here.stop % part == 0:
+            cut = (slice(None), slice(None), slice(here.stop - part, here.stop))
+            copies.append(
+                pltpu.make_async_copy(out_ref.at[cut], out_hbm.at[cut], sems.at[len(copies)])
+            )
+            copies[-1].start()
 
     correct(size, length, features, weight_refs, finish)
+    for copy in copies:
+        copy.wait()
 
 
 def selections():
@@ -294,7 +336,7 @@
 
 
 def prepare(pick_ref, stem_ref, conv_ref, gain_ref, up_ref, down_ref, out_ref, *refs):
-    inner_refs, outer_refs, (gain_out, up_out, down_out) = refs[0:2], refs[2:4], refs[4:7]
+    inner_refs, outer_refs, (up_out, down_out) = refs[0:2], refs[2:4], refs[4:6]
     section = lax.axis_index("section")
 
     def turned(left, right):
@@ -316,11 +358,12 @@
         mix_out[...] = rows[:, :80].astype(BF16)
         fix_out[0] = (conv[:, 0:1] * parts[4])[:, :16].astype(BF16)
         fix_out[1] = (conv[:, 2:3] * parts[5])[:, :16].astype(BF16)
-    gain_out[...] = jnp.sum(unit(128) * gain_ref[...], axis=1, keepdims=True)
-    up_out[...] = turned(up_ref[0], unit(128).astype(BF16)).astype(BF16)
-    down = 0.5 * lax.dot_general(
+    up = turned(up_ref[0], unit(128).astype(BF16))
+    up_out[...] = (up * (GELU_SCALE * gain_ref[...])).astype(BF16)
+    down = lax.dot_general(
         out_ref[...], down_ref[0], (((0,), (1,)), ((), ())), preferred_element_type=F32
     )
+    down = (0.5 / GELU_SCALE) * down
     down_out[...] = jnp.concatenate([down, down - down.astype(BF16).astype(F32)], axis=0).astype(BF16)
 
 
@@ -349,15 +392,29 @@
         return pairs + [(b, a) for a, b in pairs]
 
     swept, narrow = pl.pallas_call(
-        functools.partial(sweep_x, size // 128),
+        functools.partial(sweep_x, length // 128),
+        in_specs=[pl.BlockSpec(memory_space=pltpu.HBM)] * 4,
         out_shape=(shape((8, length), F32), shape((8, length), BF16)),
+        scratch_shapes=[
+            pltpu.VMEM((128, 768), BF16),
+            pltpu.VMEM((2, 4, length), F32),
+            pltpu.VMEM((4, length), F32),
+            pltpu.VMEM((2, 4, length), jnp.int32),
+            pltpu.SemaphoreType.DMA,
+            pltpu.SemaphoreType.DMA((1, 3)),
+        ],
         compiler_params=params(),
         name="sweep_x",
-    )(jnp.asarray(band_matrix(), BF16), potential, speed_x, sign_x)
+    )(
+        *(
+            pltpu.with_memory_space_constraint(value, pltpu.HBM)
+            for value in (jnp.asarray(band_matrix(), BF16), potential, speed_x, sign_x)
+        )
+    )
     far = lax.ppermute(narrow, BOTH, swaps(1))
     chip = lax.ppermute(swept, BOTH, swaps(0))
     mix_shapes = (shape((136, 80), BF16), shape((2, 128, 16), BF16))
-    shared_shapes = (shape((128, 1), F32), shape((256, 128), BF16), shape((8, 256), BF16))
+    shared_shapes = (shape((256, 128), BF16), shape((8, 256), BF16))
     made = pl.pallas_call(
         prepare,
         out_shape=mix_shapes + mix_shapes + shared_shapes,
@@ -399,7 +456,7 @@
         [(2 * w, 2 * w - 1) for w in range(1, blocks)]
         + [(2 * w + 1, 2 * w + 2) for w in range(blocks - 1)],
     )
-    inner_weights, outer_weights = made[0:2] + made[4:7], made[2:7]
+    inner_weights, outer_weights = made[0:2] + made[4:6], made[2:6]
     scratch = [pltpu.VMEM((16, length + 2 * HALO), BF16)]
     row = pl.pallas_call(
         functools.partial(correct_inner, chunk),
@@ -411,7 +468,9 @@
     return pl.pallas_call(
         functools.partial(correct_outer, chunk),
         out_shape=shape((4, 2, length), F32),
-        scratch_shapes=scratch,
+        out_specs=pl.BlockSpec(memory_space=pltpu.HBM),
+        scratch_shapes=scratch
+        + [pltpu.VMEM((4, 2, length), F32), pltpu.SemaphoreType.DMA((min(8, length // chunk),))],
         compiler_params=params(),
         name="correct_outer",
     )(outer, swap, edge, cross, own_rows, row, *outer_weights)

time: 49.8 us -> 47.2 us (0.948)
  local copies, waits for them, and re-layouts: 4.14 us -> 0.19 us
  Pallas kernels: 15.4 us -> 16.6 us
    unnamed x31 -> x23, local copies, waits for them, and re-layouts: 4.14 us -> 0.19 us
    pallas_call x1, Pallas kernels: 0.65 us -> 2.07 us  [shards(): pl.pallas_call(functools.partial(sweep_x, length // 128), in_specs=[pl.Bl...]
  transfers between devices with their start and end apart: 5 -> 5, of which waited for: 1 -> 1; matrix products, arithmetic and copies ran while one was open for 0% -> 0% of each run, Pallas kernels for 14% -> 15%
where the time goes in v4:
time: 47.2 us; the launch traced here: 46.5 us
  starting transfers between devices  24.9 us (53%)
  Pallas kernels  16.6 us (35%)
  waiting for transfers between devices  4.44 us (9%)
    ppermute x1, starting transfers between devices, shards(): lax.ppermute(cross, BOTH, [(2 * w, 2 * w - 1) for w in range(1, blocks)]...  11.8 us
    pallas_call x1, Pallas kernels, shards(): pl.pallas_call(functools.partial(correct_outer, chunk), out_shape=shape((...  7.03 us
    ppermute x1, starting transfers between devices, shards(): swap = lax.ppermute(given, 'section', [(0, 1), (1, 0)])  6.77 us
    pallas_call x1, Pallas kernels, shards(): pl.pallas_call(functools.partial(correct_inner, chunk), out_shape=shape((...  6.3 us
    ppermute x1, waiting for transfers between devices, shards(): far = lax.ppermute(narrow, BOTH, swaps(1))  4.43 us
    ppermute x1, starting transfers between devices, shards(): far = lax.ppermute(narrow, BOTH, swaps(1))  3.44 us
    ppermute x1, starting transfers between devices, shards(): lax.ppermute(edge, BOTH, [(2 * w + 1, 2 * w - 1) for w in range(1, blocks...  2.17 us
    pallas_call x1, Pallas kernels, shards(): pl.pallas_call(functools.partial(sweep_x, length // 128), in_specs=[pl.Bl...  2.07 us
  transfers between devices with their start and end apart: 5, of which 1 were waited for; matrix products, arithmetic and copies ran while one was open for 0% of the time, Pallas kernels for 15%

profile of v4, /device:TPU:7, one launch (start us, length us, event | category | flops | bytes accessed | tf_op | source)
XLA Modules:
  0.0 46.5 jit_solution(62317751284792189)
XLA Ops:
  0.0 0.0 copy-start.1
  0.0 0.0 copy-start.10
  0.0 0.0 copy-start.4
  0.0 0.0 copy-start.5
  0.0 0.0 copy-start.7
  0.0 0.0 copy-start.8
  0.0 0.0 copy-start.9
  0.0 0.0 copy-start
  0.1 0.0 copy-start.3
  0.1 2.1 %sweep_x.1 = (f32[8,16384]{1,0:T(8,128)S(1)}, bf16[8,16384]{1,0:T(8,128)(2,1)S(1)}) custom-call(bf16[128,768]{1,0:T(8,128)(2,1)} %constant.6.clone.band_hbm, f32[2,4,16384]{2,1,0:T(4,128)} %pot_hbm.1, f32[4,16384]{1,0:T(4,128)} %speed_hbm.1, s32[2,4,16384]{2,1,0:T(4,128)} %sign_hbm.1), custom_call_target="tpu_custom_call" | custom-call | tf_op jit(solution)/shard_map/sweep_x/pallas_call | solution.py:394
  2.1 0.0 copy-start.2
  2.2 0.8 %collective-permute-start = (f32[8,16384]{1,0:T(8,128)S(1)}, f32[8,16384]{1,0:T(8,128)S(1)}, u32[]{:S(2)}, u32[]{:S(2)}) collective-permute-start(f32[8,16384]{1,0:T(8,128)S(1)} %get-tuple-element.27.own_ref), channel_id=1, source_target_pairs={{0,2},{1,3},{4,6},{5,7},{8,10},{9,11},{12,14},{13,15},{16,18},{17,... | collective-permute-start | bytes 1572872 | tf_op jit(solution)/shard_map/ppermute | solution.py:415
  2.9 3.4 %collective-permute-start.1 = (bf16[8,16384]{1,0:T(8,128)(2,1)S(1)}, bf16[8,16384]{1,0:T(8,128)(2,1)S(1)}, u32[]{:S(2)}, u32[]{:S(2)}) collective-permute-start(bf16[8,16384]{1,0:T(8,128)(2,1)S(1)} %get-tuple-element.28), channel_id=1, source_target_pairs={{2,4},{3,5},{6,8},{7,9},{10,12},{11,13},{14,16},{15,17},{18,20},{1... | collective-permute-start | bytes 786440 | tf_op jit(solution)/shard_map/ppermute | solution.py:414
  6.4 0.0 copy-done.10
  6.4 0.1 copy.16.out_ref
  6.5 0.0 copy-done.1
  6.5 0.0 copy-done.4
  6.5 0.0 copy-done.5
  6.5 0.0 copy-done.7
  6.5 0.0 copy-done.8
  6.6 0.0 copy-done.9
  6.6 0.0 copy-start.6
  6.6 0.5 prepare.1
  7.0 4.4 %collective-permute-done.1.far_ref = bf16[8,16384]{1,0:T(8,128)(2,1)S(1)} collective-permute-done((bf16[8,16384]{1,0:T(8,128)(2,1)S(1)}, bf16[8,16384]{1,0:T(8,128)(2,1)S(1)}, u32[]{:S(2)}, u32[]{:S(2)}) %collective-permute-start.1) | collective-permute-done | bytes 262176 | tf_op jit(solution)/shard_map/ppermute | solution.py:414
  11.5 0.0 collective-permute-done.chip_ref
  11.5 0.0 copy-done
  11.5 0.0 copy-done.3
  11.5 0.0 copy-done.2
  11.5 0.0 copy-done.6
  11.5 0.7 %sweep_y.1 = (f32[4,16384]{1,0:T(4,128)S(1)}, bf16[16,16384]{1,0:T(8,128)(2,1)S(1)}, bf16[16,16384]{1,0:T(8,128)(2,1)S(1)}, bf16[3,2,16384]{2,1,0:T(2,128)(2,1)S...) custom-call(bf16[2,2,56,64]{3,2,1,0:T(8,128)(2,1)S(1)} %copy-done.6, ...), custom_call_target="tpu_custom_call" | custom-call | tf_op jit(solution)/shard_map/sweep_y/pallas_call | solution.py:433
  12.3 6.8 %collective-permute-start.2 = (bf16[3,2,16384]{2,1,0:T(2,128)(2,1)S(1)}, bf16[3,2,16384]{2,1,0:T(2,128)(2,1)S(1)}, u32[]{:S(2)}, u32[]{:S(2)}) collective-permute-start(bf16[3,2,16384]{2,1,0:T(2,128)(2,1)S(1)} %get-tuple-element.38), channel_id=1, source_target_pairs={{0,1},{1,0},{2,3},{3,2},{4,5},{5,4},{6,7},{7,6},{8,9},{9,8},{10,11... | collective-permute-start | bytes 589832 | tf_op jit(solution)/shard_map/ppermute | solution.py:446
  19.0 2.2 %collective-permute-start.3 = (bf16[4,16384]{1,0:T(4,128)(2,1)S(1)}, bf16[4,16384]{1,0:T(4,128)(2,1)S(1)}, u32[]{:S(2)}, u32[]{:S(2)}) collective-permute-start(bf16[4,16384]{1,0:T(4,128)(2,1)S(1)} %get-tuple-element.39), channel_id=1, source_target_pairs={{3,1},{5,3},{7,5},{9,7},{11,9},{13,11},{15,13},{17,15},{19,17},{21... | collective-permute-start | bytes 393224 | tf_op jit(solution)/shard_map/ppermute | solution.py:447
  21.2 11.8 %collective-permute-start.4 = (bf16[2,16384]{1,0:T(2,128)(2,1)S(1)}, bf16[2,16384]{1,0:T(2,128)(2,1)S(1)}, u32[]{:S(2)}, u32[]{:S(2)}) collective-permute-start(bf16[2,16384]{1,0:T(2,128)(2,1)S(1)} %get-tuple-element.40), channel_id=1, source_target_pairs={{2,1},{4,3},{6,5},{8,7},{10,9},{12,11},{14,13},{16,15},{18,17},{20... | collective-permute-start | bytes 196616 | tf_op jit(solution)/shard_map/ppermute | solution.py:453
  33.0 0.0 collective-permute-done.2.swap_ref
  33.0 6.3 %correct_inner.1.row_ref = f32[4,16384]{1,0:T(4,128)S(1)} custom-call(bf16[16,16384]{1,0:T(8,128)(2,1)S(1)} %get-tuple-element.42.inner_ref, bf16[3,2,16384]{2,1,0:T(2,128)(2,1)S(1)} %collective-permute-done.2.swap_ref, f32[4,16384]{1,0:T(4,128)S(1)} %get-tuple-element.41.own_rows_ref, bf16[136,80]{1,0:T(8,128)(2,1)S(1)} %get-tuple-element.43.refs_0_, ...), custom_call_target="tpu_custom_call" | custom-call | tf_op jit(solution)/shard_map/correct_inner/pallas_call | solution.py:461
  39.3 0.0 collective-permute-done.4.cross_ref
  39.3 0.0 collective-permute-done.3.edge_ref
  39.3 7.0 %correct_outer.1 = f32[4,2,16384]{2,1,0:T(2,128)} custom-call(bf16[16,16384]{1,0:T(8,128)(2,1)S(1)} %get-tuple-element.37.outer_ref, bf16[3,2,16384]{2,1,0:T(2,128)(2,1)S(1)} %collective-permute-done.2.swap_ref, bf16[4,16384]{1,0:T(4,128)(2,1)S(1)} %collective-permute-done.3.edge_ref, bf16[2,16384]{1,0:T(2,128)(2,1)S(1)} %collective-permute-done.4.cross_ref, ...), custom_call_target="tpu_custom_call" | custom-call | tf_op jit(solution)/shard_map/correct_outer/pallas_call | solution.py:468
Async XLA Ops:
  0.0 6.5 %copy-start.1 = (bf16[2,2,45,768]{3,2,1,0:T(8,128)(2,1)S(1)}, bf16[2,2,45,768]{3,2,1,0:T(8,128)(2,1)}, u32[]{:S(2)}) copy-start(bf16[2,2,45,768]{3,2,1,0:T(8,128)(2,1)} %constant.7.clone.pick_ref) | copy-start | bytes 829444
  0.0 6.4 %copy-start.10 = (bf16[128,4]{0,1:T(4,128)(2,1)S(1)}, bf16[128,4]{0,1:T(4,128)(2,1)}, u32[]{:S(2)}) copy-start(bf16[128,4]{0,1:T(4,128)(2,1)} %param.26) | copy-start | bytes 3076
  0.0 6.5 %copy-start.4 = (bf16[1,128,256]{2,1,0:T(8,128)(2,1)S(1)}, bf16[1,128,256]{2,1,0:T(8,128)(2,1)}, u32[]{:S(2)}) copy-start(bf16[1,128,256]{2,1,0:T(8,128)(2,1)} %up_ref.1) | copy-start | bytes 196612
  0.0 6.5 %copy-start.5 = (bf16[1,256,128]{2,1,0:T(8,128)(2,1)S(1)}, bf16[1,256,128]{2,1,0:T(8,128)(2,1)}, u32[]{:S(2)}) copy-start(bf16[1,256,128]{2,1,0:T(8,128)(2,1)} %down_ref.1) | copy-start | bytes 196612
  0.0 6.5 %copy-start.7 = (bf16[45,128]{1,0:T(8,128)(2,1)S(1)}, bf16[45,128]{1,0:T(8,128)(2,1)}, u32[]{:S(2)}) copy-start(bf16[45,128]{1,0:T(8,128)(2,1)} %stem_ref.1) | copy-start | bytes 34564
  0.0 6.5 %copy-start.8 = (bf16[1,3,128]{2,1,0:T(4,128)(2,1)S(1)}, bf16[1,3,128]{2,1,0:T(4,128)(2,1)}, u32[]{:S(2)}) copy-start(bf16[1,3,128]{2,1,0:T(4,128)(2,1)} %conv_ref.1) | copy-start | bytes 2308
  0.0 6.5 %copy-start.9 = (f32[1,128]{1,0:T(1,128)S(1)}, f32[1,128]{1,0:T(1,128)}, u32[]{:S(2)}) copy-start(f32[1,128]{1,0:T(1,128)} %gain_ref.1) | copy-start | bytes 1540
  0.0 11.4 %copy-start = (s32[2,4,16384]{2,1,0:T(4,128)S(1)}, s32[2,4,16384]{2,1,0:T(4,128)}, u32[]{:S(2)}) copy-start(s32[2,4,16384]{2,1,0:T(4,128)} %sign_ref.1) | copy-start | bytes 1572868
  0.1 11.4 %copy-start.3 = (f32[4,16384]{1,0:T(4,128)S(1)}, f32[4,16384]{1,0:T(4,128)}, u32[]{:S(2)}) copy-start(f32[4,16384]{1,0:T(4,128)} %density_ref.1) | copy-start | bytes 786436
  2.1 9.3 %copy-start.2 = (f32[4,16384]{1,0:T(4,128)S(1)}, f32[4,16384]{1,0:T(4,128)}, u32[]{:S(2)}) copy-start(f32[4,16384]{1,0:T(4,128)} %speed_ref.1) | copy-start | bytes 786436
  2.2 9.3 %collective-permute-start = (f32[8,16384]{1,0:T(8,128)S(1)}, f32[8,16384]{1,0:T(8,128)S(1)}, u32[]{:S(2)}, u32[]{:S(2)}) collective-permute-start(f32[8,16384]{1,0:T(8,128)S(1)} %get-tuple-element.27.own_ref), channel_id=1, source_target_pairs={{0,2},{1,3},{4,6},{5,7},{8,10},{9,11},{12,14},{13,15},{16,18},{17,... | collective-permute-start | bytes 1572872 | tf_op jit(solution)/shard_map/ppermute | solution.py:415
  2.9 8.6 %collective-permute-start.1 = (bf16[8,16384]{1,0:T(8,128)(2,1)S(1)}, bf16[8,16384]{1,0:T(8,128)(2,1)S(1)}, u32[]{:S(2)}, u32[]{:S(2)}) collective-permute-start(bf16[8,16384]{1,0:T(8,128)(2,1)S(1)} %get-tuple-element.28), channel_id=1, source_target_pairs={{2,4},{3,5},{6,8},{7,9},{10,12},{11,13},{14,16},{15,17},{18,20},{1... | collective-permute-start | bytes 786440 | tf_op jit(solution)/shard_map/ppermute | solution.py:414
  6.6 4.9 %copy-start.6 = (bf16[2,2,56,64]{3,2,1,0:T(8,128)(2,1)S(1)}, bf16[2,2,56,64]{3,2,1,0:T(8,128)(2,1)}, u32[]{:S(2)}) copy-start(bf16[2,2,56,64]{3,2,1,0:T(8,128)(2,1)} %constant.8.clone.column_ref) | copy-start | bytes 86020
  12.3 20.7 %collective-permute-start.2 = (bf16[3,2,16384]{2,1,0:T(2,128)(2,1)S(1)}, bf16[3,2,16384]{2,1,0:T(2,128)(2,1)S(1)}, u32[]{:S(2)}, u32[]{:S(2)}) collective-permute-start(bf16[3,2,16384]{2,1,0:T(2,128)(2,1)S(1)} %get-tuple-element.38), channel_id=1, source_target_pairs={{0,1},{1,0},{2,3},{3,2},{4,5},{5,4},{6,7},{7,6},{8,9},{9,8},{10,11... | collective-permute-start | bytes 589832 | tf_op jit(solution)/shard_map/ppermute | solution.py:446
  19.0 20.3 %collective-permute-start.3 = (bf16[4,16384]{1,0:T(4,128)(2,1)S(1)}, bf16[4,16384]{1,0:T(4,128)(2,1)S(1)}, u32[]{:S(2)}, u32[]{:S(2)}) collective-permute-start(bf16[4,16384]{1,0:T(4,128)(2,1)S(1)} %get-tuple-element.39), channel_id=1, source_target_pairs={{3,1},{5,3},{7,5},{9,7},{11,9},{13,11},{15,13},{17,15},{19,17},{21... | collective-permute-start | bytes 393224 | tf_op jit(solution)/shard_map/ppermute | solution.py:447
  21.2 18.1 %collective-permute-start.4 = (bf16[2,16384]{1,0:T(2,128)(2,1)S(1)}, bf16[2,16384]{1,0:T(2,128)(2,1)S(1)}, u32[]{:S(2)}, u32[]{:S(2)}) collective-permute-start(bf16[2,16384]{1,0:T(2,128)(2,1)S(1)} %get-tuple-element.40), channel_id=1, source_target_pairs={{2,1},{4,3},{6,5},{8,7},{10,9},{12,11},{14,13},{16,15},{18,17},{20... | collective-permute-start | bytes 196616 | tf_op jit(solution)/shard_map/ppermute | solution.py:453

commit v5 on v4

--- a/solution.py
+++ b/solution.py
@@ -383,7 +383,7 @@
 ):
     length = potential.shape[2]
     size = min(length, 2048)
-    chunk = min(length, 512)
+    chunk = min(length, 1024)
     blocks = lax.axis_size("wide")
     shape = jax.ShapeDtypeStruct
 

time: 47.2 us -> 45.5 us (0.964)
  Pallas kernels: 16.6 us -> 14.9 us
    pallas_call x1, Pallas kernels: 6.3 us -> 5.44 us  [shards(): pl.pallas_call(functools.partial(correct_inner, chunk), out_shape=shape((...]
    pallas_call x1, Pallas kernels: 7.03 us -> 6.2 us  [shards(): pl.pallas_call(functools.partial(correct_outer, chunk), out_shape=shape((...]
  transfers between devices with their start and end apart: 5 -> 5, of which waited for: 1 -> 1; matrix products, arithmetic and copies ran while one was open for 0% -> 0% of each run, Pallas kernels for 15% -> 13%
where the time goes in v5:
time: 45.5 us; the launch traced here: 44.8 us
  starting transfers between devices  24.9 us (55%)
  Pallas kernels  14.9 us (33%)
  waiting for transfers between devices  4.44 us (10%)
    ppermute x1, starting transfers between devices, shards(): lax.ppermute(cross, BOTH, [(2 * w, 2 * w - 1) for w in range(1, blocks)]...  11.8 us
    ppermute x1, starting transfers between devices, shards(): swap = lax.ppermute(given, 'section', [(0, 1), (1, 0)])  6.77 us
    pallas_call x1, Pallas kernels, shards(): pl.pallas_call(functools.partial(correct_outer, chunk), out_shape=shape((...  6.2 us
    pallas_call x1, Pallas kernels, shards(): pl.pallas_call(functools.partial(correct_inner, chunk), out_shape=shape((...  5.44 us
    ppermute x1, waiting for transfers between devices, shards(): far = lax.ppermute(narrow, BOTH, swaps(1))  4.43 us
    ppermute x1, starting transfers between devices, shards(): far = lax.ppermute(narrow, BOTH, swaps(1))  3.44 us
    ppermute x1, starting transfers between devices, shards(): lax.ppermute(edge, BOTH, [(2 * w + 1, 2 * w - 1) for w in range(1, blocks...  2.17 us
    pallas_call x1, Pallas kernels, shards(): pl.pallas_call(functools.partial(sweep_x, length // 128), in_specs=[pl.Bl...  2.07 us
  transfers between devices with their start and end apart: 5, of which 1 were waited for; matrix products, arithmetic and copies ran while one was open for 0% of the time, Pallas kernels for 13%

profile of v5, /device:TPU:7, one launch (start us, length us, event | category | flops | bytes accessed | tf_op | source)
XLA Modules:
  0.0 44.8 jit_solution(16732080840658225172)
XLA Ops:
  0.0 0.0 copy-start.1
  0.0 0.0 copy-start.10
  0.0 0.0 copy-start.4
  0.0 0.0 copy-start.5
  0.0 0.0 copy-start.7
  0.0 0.0 copy-start.8
  0.0 0.0 copy-start.9
  0.0 0.0 copy-start
  0.1 0.0 copy-start.3
  0.1 2.1 %sweep_x.1 = (f32[8,16384]{1,0:T(8,128)S(1)}, bf16[8,16384]{1,0:T(8,128)(2,1)S(1)}) custom-call(bf16[128,768]{1,0:T(8,128)(2,1)} %constant.6.clone.band_hbm, f32[2,4,16384]{2,1,0:T(4,128)} %pot_hbm.1, f32[4,16384]{1,0:T(4,128)} %speed_hbm.1, s32[2,4,16384]{2,1,0:T(4,128)} %sign_hbm.1), custom_call_target="tpu_custom_call" | custom-call | tf_op jit(solution)/shard_map/sweep_x/pallas_call | solution.py:394
  2.1 0.0 copy-start.2
  2.2 0.8 %collective-permute-start = (f32[8,16384]{1,0:T(8,128)S(1)}, f32[8,16384]{1,0:T(8,128)S(1)}, u32[]{:S(2)}, u32[]{:S(2)}) collective-permute-start(f32[8,16384]{1,0:T(8,128)S(1)} %get-tuple-element.27.own_ref), channel_id=1, source_target_pairs={{0,2},{1,3},{4,6},{5,7},{8,10},{9,11},{12,14},{13,15},{16,18},{17,... | collective-permute-start | bytes 1572872 | tf_op jit(solution)/shard_map/ppermute | solution.py:415
  2.9 3.4 %collective-permute-start.1 = (bf16[8,16384]{1,0:T(8,128)(2,1)S(1)}, bf16[8,16384]{1,0:T(8,128)(2,1)S(1)}, u32[]{:S(2)}, u32[]{:S(2)}) collective-permute-start(bf16[8,16384]{1,0:T(8,128)(2,1)S(1)} %get-tuple-element.28), channel_id=1, source_target_pairs={{2,4},{3,5},{6,8},{7,9},{10,12},{11,13},{14,16},{15,17},{18,20},{1... | collective-permute-start | bytes 786440 | tf_op jit(solution)/shard_map/ppermute | solution.py:414
  6.4 0.0 copy-done.10
  6.4 0.1 copy.16.out_ref
  6.5 0.0 copy-done.1
  6.5 0.0 copy-done.4
  6.5 0.0 copy-done.5
  6.5 0.0 copy-done.7
  6.5 0.0 copy-done.8
  6.6 0.0 copy-done.9
  6.6 0.0 copy-start.6
  6.6 0.5 %prepare.1 = (bf16[136,80]{1,0:T(8,128)(2,1)S(1)}, bf16[2,128,16]{2,1,0:T(8,128)(2,1)S(1)}, bf16[136,80]{1,0:T(8,128)(2,1)S(1)}, bf16[2,128,16]{2,1,0:T(8,128)(2...) custom-call(bf16[2,2,45,768]{3,2,1,0:T(8,128)(2,1)S(1)} %copy-done.1, bf16[45,128]{1,0:T(8,128)(2,1)S(1)} %copy-done.7, ...), custom_call_target="tpu_custom_call" | custom-call | tf_op jit(solution)/shard_map/prepare/pallas_call | solution.py:418
  7.0 4.4 %collective-permute-done.1.far_ref = bf16[8,16384]{1,0:T(8,128)(2,1)S(1)} collective-permute-done((bf16[8,16384]{1,0:T(8,128)(2,1)S(1)}, bf16[8,16384]{1,0:T(8,128)(2,1)S(1)}, u32[]{:S(2)}, u32[]{:S(2)}) %collective-permute-start.1) | collective-permute-done | bytes 262176 | tf_op jit(solution)/shard_map/ppermute | solution.py:414
  11.5 0.0 collective-permute-done.chip_ref
  11.5 0.0 copy-done
  11.5 0.0 copy-done.3
  11.5 0.0 copy-done.2
  11.5 0.0 copy-done.6
  11.5 0.7 %sweep_y.1 = (f32[4,16384]{1,0:T(4,128)S(1)}, bf16[16,16384]{1,0:T(8,128)(2,1)S(1)}, bf16[16,16384]{1,0:T(8,128)(2,1)S(1)}, bf16[3,2,16384]{2,1,0:T(2,128)(2,1)S...) custom-call(bf16[2,2,56,64]{3,2,1,0:T(8,128)(2,1)S(1)} %copy-done.6, ...), custom_call_target="tpu_custom_call" | custom-call | tf_op jit(solution)/shard_map/sweep_y/pallas_call | solution.py:433
  12.3 6.8 %collective-permute-start.2 = (bf16[3,2,16384]{2,1,0:T(2,128)(2,1)S(1)}, bf16[3,2,16384]{2,1,0:T(2,128)(2,1)S(1)}, u32[]{:S(2)}, u32[]{:S(2)}) collective-permute-start(bf16[3,2,16384]{2,1,0:T(2,128)(2,1)S(1)} %get-tuple-element.38), channel_id=1, source_target_pairs={{0,1},{1,0},{2,3},{3,2},{4,5},{5,4},{6,7},{7,6},{8,9},{9,8},{10,11... | collective-permute-start | bytes 589832 | tf_op jit(solution)/shard_map/ppermute | solution.py:446
  19.0 2.2 %collective-permute-start.3 = (bf16[4,16384]{1,0:T(4,128)(2,1)S(1)}, bf16[4,16384]{1,0:T(4,128)(2,1)S(1)}, u32[]{:S(2)}, u32[]{:S(2)}) collective-permute-start(bf16[4,16384]{1,0:T(4,128)(2,1)S(1)} %get-tuple-element.39), channel_id=1, source_target_pairs={{3,1},{5,3},{7,5},{9,7},{11,9},{13,11},{15,13},{17,15},{19,17},{21... | collective-permute-start | bytes 393224 | tf_op jit(solution)/shard_map/ppermute | solution.py:447
  21.2 11.8 %collective-permute-start.4 = (bf16[2,16384]{1,0:T(2,128)(2,1)S(1)}, bf16[2,16384]{1,0:T(2,128)(2,1)S(1)}, u32[]{:S(2)}, u32[]{:S(2)}) collective-permute-start(bf16[2,16384]{1,0:T(2,128)(2,1)S(1)} %get-tuple-element.40), channel_id=1, source_target_pairs={{2,1},{4,3},{6,5},{8,7},{10,9},{12,11},{14,13},{16,15},{18,17},{20... | collective-permute-start | bytes 196616 | tf_op jit(solution)/shard_map/ppermute | solution.py:453
  33.0 0.0 collective-permute-done.2.swap_ref
  33.0 5.4 %correct_inner.1.row_ref = f32[4,16384]{1,0:T(4,128)S(1)} custom-call(bf16[16,16384]{1,0:T(8,128)(2,1)S(1)} %get-tuple-element.42.inner_ref, bf16[3,2,16384]{2,1,0:T(2,128)(2,1)S(1)} %collective-permute-done.2.swap_ref, f32[4,16384]{1,0:T(4,128)S(1)} %get-tuple-element.41.own_rows_ref, bf16[136,80]{1,0:T(8,128)(2,1)S(1)} %get-tuple-element.43.refs_0_, ...), custom_call_target="tpu_custom_call" | custom-call | tf_op jit(solution)/shard_map/correct_inner/pallas_call | solution.py:461
  38.4 0.0 collective-permute-done.4.cross_ref
  38.4 0.0 collective-permute-done.3.edge_ref
  38.5 6.2 %correct_outer.1 = f32[4,2,16384]{2,1,0:T(2,128)} custom-call(bf16[16,16384]{1,0:T(8,128)(2,1)S(1)} %get-tuple-element.37.outer_ref, bf16[3,2,16384]{2,1,0:T(2,128)(2,1)S(1)} %collective-permute-done.2.swap_ref, bf16[4,16384]{1,0:T(4,128)(2,1)S(1)} %collective-permute-done.3.edge_ref, bf16[2,16384]{1,0:T(2,128)(2,1)S(1)} %collective-permute-done.4.cross_ref, ...), custom_call_target="tpu_custom_call" | custom-call | tf_op jit(solution)/shard_map/correct_outer/pallas_call | solution.py:468
Async XLA Ops:
  0.0 6.5 %copy-start.1 = (bf16[2,2,45,768]{3,2,1,0:T(8,128)(2,1)S(1)}, bf16[2,2,45,768]{3,2,1,0:T(8,128)(2,1)}, u32[]{:S(2)}) copy-start(bf16[2,2,45,768]{3,2,1,0:T(8,128)(2,1)} %constant.7.clone.pick_ref) | copy-start | bytes 829444
  0.0 6.4 %copy-start.10 = (bf16[128,4]{0,1:T(4,128)(2,1)S(1)}, bf16[128,4]{0,1:T(4,128)(2,1)}, u32[]{:S(2)}) copy-start(bf16[128,4]{0,1:T(4,128)(2,1)} %param.26) | copy-start | bytes 3076
  0.0 6.5 %copy-start.4 = (bf16[1,128,256]{2,1,0:T(8,128)(2,1)S(1)}, bf16[1,128,256]{2,1,0:T(8,128)(2,1)}, u32[]{:S(2)}) copy-start(bf16[1,128,256]{2,1,0:T(8,128)(2,1)} %up_ref.1) | copy-start | bytes 196612
  0.0 6.5 %copy-start.5 = (bf16[1,256,128]{2,1,0:T(8,128)(2,1)S(1)}, bf16[1,256,128]{2,1,0:T(8,128)(2,1)}, u32[]{:S(2)}) copy-start(bf16[1,256,128]{2,1,0:T(8,128)(2,1)} %down_ref.1) | copy-start | bytes 196612
  0.0 6.5 %copy-start.7 = (bf16[45,128]{1,0:T(8,128)(2,1)S(1)}, bf16[45,128]{1,0:T(8,128)(2,1)}, u32[]{:S(2)}) copy-start(bf16[45,128]{1,0:T(8,128)(2,1)} %stem_ref.1) | copy-start | bytes 34564
  0.0 6.5 %copy-start.8 = (bf16[1,3,128]{2,1,0:T(4,128)(2,1)S(1)}, bf16[1,3,128]{2,1,0:T(4,128)(2,1)}, u32[]{:S(2)}) copy-start(bf16[1,3,128]{2,1,0:T(4,128)(2,1)} %conv_ref.1) | copy-start | bytes 2308
  0.0 6.5 %copy-start.9 = (f32[1,128]{1,0:T(1,128)S(1)}, f32[1,128]{1,0:T(1,128)}, u32[]{:S(2)}) copy-start(f32[1,128]{1,0:T(1,128)} %gain_ref.1) | copy-start | bytes 1540
  0.0 11.4 %copy-start = (s32[2,4,16384]{2,1,0:T(4,128)S(1)}, s32[2,4,16384]{2,1,0:T(4,128)}, u32[]{:S(2)}) copy-start(s32[2,4,16384]{2,1,0:T(4,128)} %sign_ref.1) | copy-start | bytes 1572868
  0.1 11.4 %copy-start.3 = (f32[4,16384]{1,0:T(4,128)S(1)}, f32[4,16384]{1,0:T(4,128)}, u32[]{:S(2)}) copy-start(f32[4,16384]{1,0:T(4,128)} %density_ref.1) | copy-start | bytes 786436
  2.1 9.3 %copy-start.2 = (f32[4,16384]{1,0:T(4,128)S(1)}, f32[4,16384]{1,0:T(4,128)}, u32[]{:S(2)}) copy-start(f32[4,16384]{1,0:T(4,128)} %speed_ref.1) | copy-start | bytes 786436
  2.2 9.3 %collective-permute-start = (f32[8,16384]{1,0:T(8,128)S(1)}, f32[8,16384]{1,0:T(8,128)S(1)}, u32[]{:S(2)}, u32[]{:S(2)}) collective-permute-start(f32[8,16384]{1,0:T(8,128)S(1)} %get-tuple-element.27.own_ref), channel_id=1, source_target_pairs={{0,2},{1,3},{4,6},{5,7},{8,10},{9,11},{12,14},{13,15},{16,18},{17,... | collective-permute-start | bytes 1572872 | tf_op jit(solution)/shard_map/ppermute | solution.py:415
  2.9 8.6 %collective-permute-start.1 = (bf16[8,16384]{1,0:T(8,128)(2,1)S(1)}, bf16[8,16384]{1,0:T(8,128)(2,1)S(1)}, u32[]{:S(2)}, u32[]{:S(2)}) collective-permute-start(bf16[8,16384]{1,0:T(8,128)(2,1)S(1)} %get-tuple-element.28), channel_id=1, source_target_pairs={{2,4},{3,5},{6,8},{7,9},{10,12},{11,13},{14,16},{15,17},{18,20},{1... | collective-permute-start | bytes 786440 | tf_op jit(solution)/shard_map/ppermute | solution.py:414
  6.6 4.9 %copy-start.6 = (bf16[2,2,56,64]{3,2,1,0:T(8,128)(2,1)S(1)}, bf16[2,2,56,64]{3,2,1,0:T(8,128)(2,1)}, u32[]{:S(2)}) copy-start(bf16[2,2,56,64]{3,2,1,0:T(8,128)(2,1)} %constant.8.clone.column_ref) | copy-start | bytes 86020
  12.3 20.7 %collective-permute-start.2 = (bf16[3,2,16384]{2,1,0:T(2,128)(2,1)S(1)}, bf16[3,2,16384]{2,1,0:T(2,128)(2,1)S(1)}, u32[]{:S(2)}, u32[]{:S(2)}) collective-permute-start(bf16[3,2,16384]{2,1,0:T(2,128)(2,1)S(1)} %get-tuple-element.38), channel_id=1, source_target_pairs={{0,1},{1,0},{2,3},{3,2},{4,5},{5,4},{6,7},{7,6},{8,9},{9,8},{10,11... | collective-permute-start | bytes 589832 | tf_op jit(solution)/shard_map/ppermute | solution.py:446
  19.0 19.4 %collective-permute-start.3 = (bf16[4,16384]{1,0:T(4,128)(2,1)S(1)}, bf16[4,16384]{1,0:T(4,128)(2,1)S(1)}, u32[]{:S(2)}, u32[]{:S(2)}) collective-permute-start(bf16[4,16384]{1,0:T(4,128)(2,1)S(1)} %get-tuple-element.39), channel_id=1, source_target_pairs={{3,1},{5,3},{7,5},{9,7},{11,9},{13,11},{15,13},{17,15},{19,17},{21... | collective-permute-start | bytes 393224 | tf_op jit(solution)/shard_map/ppermute | solution.py:447
  21.2 17.2 %collective-permute-start.4 = (bf16[2,16384]{1,0:T(2,128)(2,1)S(1)}, bf16[2,16384]{1,0:T(2,128)(2,1)S(1)}, u32[]{:S(2)}, u32[]{:S(2)}) collective-permute-start(bf16[2,16384]{1,0:T(2,128)(2,1)S(1)} %get-tuple-element.40), channel_id=1, source_target_pairs={{2,1},{4,3},{6,5},{8,7},{10,9},{12,11},{14,13},{16,15},{18,17},{20... | collective-permute-start | bytes 196616 | tf_op jit(solution)/shard_map/ppermute | solution.py:453

commit v6 on v5

--- a/solution.py
+++ b/solution.py
@@ -382,7 +382,7 @@
     out_weight,
 ):
     length = potential.shape[2]
-    size = min(length, 2048)
+    size = min(length, 4096)
     chunk = min(length, 1024)
     blocks = lax.axis_size("wide")
     shape = jax.ShapeDtypeStruct
@@ -470,7 +470,7 @@
         out_shape=shape((4, 2, length), F32),
         out_specs=pl.BlockSpec(memory_space=pltpu.HBM),
         scratch_shapes=scratch
-        + [pltpu.VMEM((4, 2, length), F32), pltpu.SemaphoreType.DMA((min(8, length // chunk),))],
+        + [pltpu.VMEM((4, 2, length), F32), pltpu.SemaphoreType.DMA((length // chunk,))],
         compiler_params=params(),
         name="correct_outer",
     )(outer, swap, edge, cross, own_rows, row, *outer_weights)

time: 45.5 us -> 45.6 us (level)
  no operation moved by 1% of the time
where the time goes in v6:
time: 45.6 us; the launch traced here: 44.9 us
  starting transfers between devices  24.9 us (55%)
  Pallas kernels  15 us (33%)
  waiting for transfers between devices  4.44 us (10%)
    ppermute x1, starting transfers between devices, shards(): lax.ppermute(cross, BOTH, [(2 * w, 2 * w - 1) for w in range(1, blocks)]...  11.8 us
    ppermute x1, starting transfers between devices, shards(): swap = lax.ppermute(given, 'section', [(0, 1), (1, 0)])  6.77 us
    pallas_call x1, Pallas kernels, shards(): pl.pallas_call(functools.partial(correct_outer, chunk), out_shape=shape((...  6.27 us
    pallas_call x1, Pallas kernels, shards(): pl.pallas_call(functools.partial(correct_inner, chunk), out_shape=shape((...  5.44 us
    ppermute x1, waiting for transfers between devices, shards(): far = lax.ppermute(narrow, BOTH, swaps(1))  4.43 us
    ppermute x1, starting transfers between devices, shards(): far = lax.ppermute(narrow, BOTH, swaps(1))  3.44 us
    ppermute x1, starting transfers between devices, shards(): lax.ppermute(edge, BOTH, [(2 * w + 1, 2 * w - 1) for w in range(1, blocks...  2.17 us
    pallas_call x1, Pallas kernels, shards(): pl.pallas_call(functools.partial(sweep_x, length // 128), in_specs=[pl.Bl...  2.07 us
  transfers between devices with their start and end apart: 5, of which 1 were waited for; matrix products, arithmetic and copies ran while one was open for 0% of the time, Pallas kernels for 13%

profile of v6, /device:TPU:7, one launch (start us, length us, event | category | flops | bytes accessed | tf_op | source)
XLA Modules:
  0.0 44.9 jit_solution(17974836618249821984)
XLA Ops:
  0.0 0.0 copy-start.1
  0.0 0.0 copy-start.10
  0.0 0.0 copy-start.4
  0.0 0.0 copy-start.5
  0.0 0.0 copy-start.7
  0.0 0.0 copy-start.8
  0.0 0.0 copy-start.9
  0.0 0.0 copy-start
  0.1 0.0 copy-start.3
  0.1 2.1 %sweep_x.1 = (f32[8,16384]{1,0:T(8,128)S(1)}, bf16[8,16384]{1,0:T(8,128)(2,1)S(1)}) custom-call(bf16[128,768]{1,0:T(8,128)(2,1)} %constant.6.clone.band_hbm, f32[2,4,16384]{2,1,0:T(4,128)} %pot_hbm.1, f32[4,16384]{1,0:T(4,128)} %speed_hbm.1, s32[2,4,16384]{2,1,0:T(4,128)} %sign_hbm.1), custom_call_target="tpu_custom_call" | custom-call | tf_op jit(solution)/shard_map/sweep_x/pallas_call | solution.py:394
  2.1 0.0 copy-start.2
  2.2 0.8 %collective-permute-start = (f32[8,16384]{1,0:T(8,128)S(1)}, f32[8,16384]{1,0:T(8,128)S(1)}, u32[]{:S(2)}, u32[]{:S(2)}) collective-permute-start(f32[8,16384]{1,0:T(8,128)S(1)} %get-tuple-element.27.own_ref), channel_id=1, source_target_pairs={{0,2},{1,3},{4,6},{5,7},{8,10},{9,11},{12,14},{13,15},{16,18},{17,... | collective-permute-start | bytes 1572872 | tf_op jit(solution)/shard_map/ppermute | solution.py:415
  2.9 3.4 %collective-permute-start.1 = (bf16[8,16384]{1,0:T(8,128)(2,1)S(1)}, bf16[8,16384]{1,0:T(8,128)(2,1)S(1)}, u32[]{:S(2)}, u32[]{:S(2)}) collective-permute-start(bf16[8,16384]{1,0:T(8,128)(2,1)S(1)} %get-tuple-element.28), channel_id=1, source_target_pairs={{2,4},{3,5},{6,8},{7,9},{10,12},{11,13},{14,16},{15,17},{18,20},{1... | collective-permute-start | bytes 786440 | tf_op jit(solution)/shard_map/ppermute | solution.py:414
  6.4 0.0 copy-done.10
  6.4 0.1 copy.16.out_ref
  6.5 0.0 copy-done.1
  6.5 0.0 copy-done.4
  6.5 0.0 copy-done.5
  6.5 0.0 copy-done.7
  6.5 0.0 copy-done.8
  6.6 0.0 copy-done.9
  6.6 0.0 copy-start.6
  6.6 0.5 %prepare.1 = (bf16[136,80]{1,0:T(8,128)(2,1)S(1)}, bf16[2,128,16]{2,1,0:T(8,128)(2,1)S(1)}, bf16[136,80]{1,0:T(8,128)(2,1)S(1)}, bf16[2,128,16]{2,1,0:T(8,128)(2...) custom-call(bf16[2,2,45,768]{3,2,1,0:T(8,128)(2,1)S(1)} %copy-done.1, bf16[45,128]{1,0:T(8,128)(2,1)S(1)} %copy-done.7, ...), custom_call_target="tpu_custom_call" | custom-call | tf_op jit(solution)/shard_map/prepare/pallas_call | solution.py:418
  7.0 4.4 %collective-permute-done.1.far_ref = bf16[8,16384]{1,0:T(8,128)(2,1)S(1)} collective-permute-done((bf16[8,16384]{1,0:T(8,128)(2,1)S(1)}, bf16[8,16384]{1,0:T(8,128)(2,1)S(1)}, u32[]{:S(2)}, u32[]{:S(2)}) %collective-permute-start.1) | collective-permute-done | bytes 262176 | tf_op jit(solution)/shard_map/ppermute | solution.py:414
  11.5 0.0 collective-permute-done.chip_ref
  11.5 0.0 copy-done
  11.5 0.0 copy-done.3
  11.5 0.0 copy-done.2
  11.5 0.0 copy-done.6
  11.5 0.7 %sweep_y.1 = (f32[4,16384]{1,0:T(4,128)S(1)}, bf16[16,16384]{1,0:T(8,128)(2,1)S(1)}, bf16[16,16384]{1,0:T(8,128)(2,1)S(1)}, bf16[3,2,16384]{2,1,0:T(2,128)(2,1)S...) custom-call(bf16[2,2,56,64]{3,2,1,0:T(8,128)(2,1)S(1)} %copy-done.6, ...), custom_call_target="tpu_custom_call" | custom-call | tf_op jit(solution)/shard_map/sweep_y/pallas_call | solution.py:433
  12.3 6.8 %collective-permute-start.2 = (bf16[3,2,16384]{2,1,0:T(2,128)(2,1)S(1)}, bf16[3,2,16384]{2,1,0:T(2,128)(2,1)S(1)}, u32[]{:S(2)}, u32[]{:S(2)}) collective-permute-start(bf16[3,2,16384]{2,1,0:T(2,128)(2,1)S(1)} %get-tuple-element.38), channel_id=1, source_target_pairs={{0,1},{1,0},{2,3},{3,2},{4,5},{5,4},{6,7},{7,6},{8,9},{9,8},{10,11... | collective-permute-start | bytes 589832 | tf_op jit(solution)/shard_map/ppermute | solution.py:446
  19.0 2.2 %collective-permute-start.3 = (bf16[4,16384]{1,0:T(4,128)(2,1)S(1)}, bf16[4,16384]{1,0:T(4,128)(2,1)S(1)}, u32[]{:S(2)}, u32[]{:S(2)}) collective-permute-start(bf16[4,16384]{1,0:T(4,128)(2,1)S(1)} %get-tuple-element.39), channel_id=1, source_target_pairs={{3,1},{5,3},{7,5},{9,7},{11,9},{13,11},{15,13},{17,15},{19,17},{21... | collective-permute-start | bytes 393224 | tf_op jit(solution)/shard_map/ppermute | solution.py:447
  21.2 11.8 %collective-permute-start.4 = (bf16[2,16384]{1,0:T(2,128)(2,1)S(1)}, bf16[2,16384]{1,0:T(2,128)(2,1)S(1)}, u32[]{:S(2)}, u32[]{:S(2)}) collective-permute-start(bf16[2,16384]{1,0:T(2,128)(2,1)S(1)} %get-tuple-element.40), channel_id=1, source_target_pairs={{2,1},{4,3},{6,5},{8,7},{10,9},{12,11},{14,13},{16,15},{18,17},{20... | collective-permute-start | bytes 196616 | tf_op jit(solution)/shard_map/ppermute | solution.py:453
  33.0 0.0 collective-permute-done.2.swap_ref
  33.0 5.4 %correct_inner.1.row_ref = f32[4,16384]{1,0:T(4,128)S(1)} custom-call(bf16[16,16384]{1,0:T(8,128)(2,1)S(1)} %get-tuple-element.42.inner_ref, bf16[3,2,16384]{2,1,0:T(2,128)(2,1)S(1)} %collective-permute-done.2.swap_ref, f32[4,16384]{1,0:T(4,128)S(1)} %get-tuple-element.41.own_rows_ref, bf16[136,80]{1,0:T(8,128)(2,1)S(1)} %get-tuple-element.43.refs_0_, ...), custom_call_target="tpu_custom_call" | custom-call | tf_op jit(solution)/shard_map/correct_inner/pallas_call | solution.py:461
  38.4 0.0 collective-permute-done.4.cross_ref
  38.4 0.0 collective-permute-done.3.edge_ref
  38.5 6.3 %correct_outer.1 = f32[4,2,16384]{2,1,0:T(2,128)} custom-call(bf16[16,16384]{1,0:T(8,128)(2,1)S(1)} %get-tuple-element.37.outer_ref, bf16[3,2,16384]{2,1,0:T(2,128)(2,1)S(1)} %collective-permute-done.2.swap_ref, bf16[4,16384]{1,0:T(4,128)(2,1)S(1)} %collective-permute-done.3.edge_ref, bf16[2,16384]{1,0:T(2,128)(2,1)S(1)} %collective-permute-done.4.cross_ref, ...), custom_call_target="tpu_custom_call" | custom-call | tf_op jit(solution)/shard_map/correct_outer/pallas_call | solution.py:468
Async XLA Ops:
  0.0 6.5 %copy-start.1 = (bf16[2,2,45,768]{3,2,1,0:T(8,128)(2,1)S(1)}, bf16[2,2,45,768]{3,2,1,0:T(8,128)(2,1)}, u32[]{:S(2)}) copy-start(bf16[2,2,45,768]{3,2,1,0:T(8,128)(2,1)} %constant.7.clone.pick_ref) | copy-start | bytes 829444
  0.0 6.4 %copy-start.10 = (bf16[128,4]{0,1:T(4,128)(2,1)S(1)}, bf16[128,4]{0,1:T(4,128)(2,1)}, u32[]{:S(2)}) copy-start(bf16[128,4]{0,1:T(4,128)(2,1)} %param.26) | copy-start | bytes 3076
  0.0 6.5 %copy-start.4 = (bf16[1,128,256]{2,1,0:T(8,128)(2,1)S(1)}, bf16[1,128,256]{2,1,0:T(8,128)(2,1)}, u32[]{:S(2)}) copy-start(bf16[1,128,256]{2,1,0:T(8,128)(2,1)} %up_ref.1) | copy-start | bytes 196612
  0.0 6.5 %copy-start.5 = (bf16[1,256,128]{2,1,0:T(8,128)(2,1)S(1)}, bf16[1,256,128]{2,1,0:T(8,128)(2,1)}, u32[]{:S(2)}) copy-start(bf16[1,256,128]{2,1,0:T(8,128)(2,1)} %down_ref.1) | copy-start | bytes 196612
  0.0 6.5 %copy-start.7 = (bf16[45,128]{1,0:T(8,128)(2,1)S(1)}, bf16[45,128]{1,0:T(8,128)(2,1)}, u32[]{:S(2)}) copy-start(bf16[45,128]{1,0:T(8,128)(2,1)} %stem_ref.1) | copy-start | bytes 34564
  0.0 6.5 %copy-start.8 = (bf16[1,3,128]{2,1,0:T(4,128)(2,1)S(1)}, bf16[1,3,128]{2,1,0:T(4,128)(2,1)}, u32[]{:S(2)}) copy-start(bf16[1,3,128]{2,1,0:T(4,128)(2,1)} %conv_ref.1) | copy-start | bytes 2308
  0.0 6.5 %copy-start.9 = (f32[1,128]{1,0:T(1,128)S(1)}, f32[1,128]{1,0:T(1,128)}, u32[]{:S(2)}) copy-start(f32[1,128]{1,0:T(1,128)} %gain_ref.1) | copy-start | bytes 1540
  0.0 11.4 %copy-start = (s32[2,4,16384]{2,1,0:T(4,128)S(1)}, s32[2,4,16384]{2,1,0:T(4,128)}, u32[]{:S(2)}) copy-start(s32[2,4,16384]{2,1,0:T(4,128)} %sign_ref.1) | copy-start | bytes 1572868
  0.1 11.4 %copy-start.3 = (f32[4,16384]{1,0:T(4,128)S(1)}, f32[4,16384]{1,0:T(4,128)}, u32[]{:S(2)}) copy-start(f32[4,16384]{1,0:T(4,128)} %density_ref.1) | copy-start | bytes 786436
  2.1 9.3 %copy-start.2 = (f32[4,16384]{1,0:T(4,128)S(1)}, f32[4,16384]{1,0:T(4,128)}, u32[]{:S(2)}) copy-start(f32[4,16384]{1,0:T(4,128)} %speed_ref.1) | copy-start | bytes 786436
  2.2 9.3 %collective-permute-start = (f32[8,16384]{1,0:T(8,128)S(1)}, f32[8,16384]{1,0:T(8,128)S(1)}, u32[]{:S(2)}, u32[]{:S(2)}) collective-permute-start(f32[8,16384]{1,0:T(8,128)S(1)} %get-tuple-element.27.own_ref), channel_id=1, source_target_pairs={{0,2},{1,3},{4,6},{5,7},{8,10},{9,11},{12,14},{13,15},{16,18},{17,... | collective-permute-start | bytes 1572872 | tf_op jit(solution)/shard_map/ppermute | solution.py:415
  2.9 8.6 %collective-permute-start.1 = (bf16[8,16384]{1,0:T(8,128)(2,1)S(1)}, bf16[8,16384]{1,0:T(8,128)(2,1)S(1)}, u32[]{:S(2)}, u32[]{:S(2)}) collective-permute-start(bf16[8,16384]{1,0:T(8,128)(2,1)S(1)} %get-tuple-element.28), channel_id=1, source_target_pairs={{2,4},{3,5},{6,8},{7,9},{10,12},{11,13},{14,16},{15,17},{18,20},{1... | collective-permute-start | bytes 786440 | tf_op jit(solution)/shard_map/ppermute | solution.py:414
  6.6 4.9 %copy-start.6 = (bf16[2,2,56,64]{3,2,1,0:T(8,128)(2,1)S(1)}, bf16[2,2,56,64]{3,2,1,0:T(8,128)(2,1)}, u32[]{:S(2)}) copy-start(bf16[2,2,56,64]{3,2,1,0:T(8,128)(2,1)} %constant.8.clone.column_ref) | copy-start | bytes 86020
  12.3 20.7 %collective-permute-start.2 = (bf16[3,2,16384]{2,1,0:T(2,128)(2,1)S(1)}, bf16[3,2,16384]{2,1,0:T(2,128)(2,1)S(1)}, u32[]{:S(2)}, u32[]{:S(2)}) collective-permute-start(bf16[3,2,16384]{2,1,0:T(2,128)(2,1)S(1)} %get-tuple-element.38), channel_id=1, source_target_pairs={{0,1},{1,0},{2,3},{3,2},{4,5},{5,4},{6,7},{7,6},{8,9},{9,8},{10,11... | collective-permute-start | bytes 589832 | tf_op jit(solution)/shard_map/ppermute | solution.py:446
  19.0 19.4 %collective-permute-start.3 = (bf16[4,16384]{1,0:T(4,128)(2,1)S(1)}, bf16[4,16384]{1,0:T(4,128)(2,1)S(1)}, u32[]{:S(2)}, u32[]{:S(2)}) collective-permute-start(bf16[4,16384]{1,0:T(4,128)(2,1)S(1)} %get-tuple-element.39), channel_id=1, source_target_pairs={{3,1},{5,3},{7,5},{9,7},{11,9},{13,11},{15,13},{17,15},{19,17},{21... | collective-permute-start | bytes 393224 | tf_op jit(solution)/shard_map/ppermute | solution.py:447
  21.2 17.2 %collective-permute-start.4 = (bf16[2,16384]{1,0:T(2,128)(2,1)S(1)}, bf16[2,16384]{1,0:T(2,128)(2,1)S(1)}, u32[]{:S(2)}, u32[]{:S(2)}) collective-permute-start(bf16[2,16384]{1,0:T(2,128)(2,1)S(1)} %get-tuple-element.40), channel_id=1, source_target_pairs={{2,1},{4,3},{6,5},{8,7},{10,9},{12,11},{14,13},{16,15},{18,17},{20... | collective-permute-start | bytes 196616 | tf_op jit(solution)/shard_map/ppermute | solution.py:453
